TPU v7x, 32 devices: a whole 2x2x4 slice. The times are simulated.
32 devices in a mesh: row: 8 (over z, x), off: 4 (over y, core).
Axes of the slice: x: 2, y: 2, z: 4, core: 2. Of those that a mesh axis runs over, the one named last changes fastest.
Arguments:
- start_block: float32 [6, 1048576], P(None, ('row', 'off'))
- diagonal: float32 [1048576], P(('row', 'off')), may hold values from 2 to 6
- tile_values: float32 [8, 4, 80, 128, 128], P('row', 'off'), may hold values from -0.1875 to 0.1875
- tile_rows: int32 [8, 4, 80], P('row', 'off'), may hold values from 0 to 1023
- tile_cols: int32 [8, 4, 80], P('row', 'off'), may hold values from 0 to 1023
- tile_counts: int32 [8, 4], P('row', 'off'), may hold values from 20 to 80, as said below
- offset_map: int32 [4], replicated, may hold values from 0 to 3, as said below
Outputs:
- final_block: float32 [6, 1048576], P(None, ('row', 'off'))
- residual: float32 [6, 1048576], P(None, ('row', 'off'))
Inputs may be any that keep to these rules, and one draw needn't show every extreme that they name: `tile_counts`: live tiles of one device; some device has exactly 80. `offset_map`: each offset 0 to 3 is held by 4 / 4 off indices.
All inputs are finite; a program needn't handle non-finite values.
Results may differ from a plain program's by a relative error of at most 0.0003.
Values sent between devices are 32-bit elements; how exact they have to be, the bound alone decides.
No kernel may reach another device: no remote copies, remote signals or barrier semaphores. Data moves between devices by JAX's collectives and lax.ppermute only.
A program may use at most 64 MiB of HBM per device.

v0:
```python
import functools
import itertools

import jax
import jax.numpy as jnp
from jax import lax
from jax.experimental import pallas as pl
from jax.experimental.pallas import tpu as pltpu
from jax.sharding import PartitionSpec as P


VMEM = pl.BlockSpec(memory_space=pltpu.VMEM)
SMEM = pl.BlockSpec(memory_space=pltpu.SMEM)
MIB = 1 << 20
BF16 = jnp.bfloat16
F32 = jnp.float32


def swap(x, axis, mask):
    n = lax.axis_size(axis)
    return lax.ppermute(x, axis, [(i, i ^ mask) for i in range(n)])


def shift(x, distances):
    rows, offs = lax.axis_size("row"), lax.axis_size("off")
    if not any(distances):
        return x
    route = [
        (r * offs + o, (r + distances[o]) % rows * offs + o) for r in range(rows) for o in range(offs)
    ]
    return lax.ppermute(x, ("row", "off"), route)


def after(x, *others):
    return lax.optimization_barrier((x, *others))[0]


def bits_of(axis):
    return [1 << b for b in reversed(range(lax.axis_size(axis).bit_length() - 1))]


def gather_off(pieces, bits, hold=()):
    pieces = dict(pieces)
    for bit in bits:
        for m in list(pieces):
            source = after(pieces[m], *hold) if m and hold else pieces[m]
            pieces[m | bit] = swap(source, "off", bit)
    return [pieces[m] for m in sorted(pieces)]


def sum_step(x, axis, bit):
    return x + swap(x, axis, bit)


def pairs(vectors):
    return [(i, j) for i in range(vectors) for j in range(i + 1)]


def call(kernel, out_shape, operands, in_specs=None, limit=16, scratch=(), flops=0, **kw):
    many = isinstance(out_shape, tuple)
    moved = sum(x.size * x.dtype.itemsize for x in operands)
    return pl.pallas_call(
        kernel,
        out_shape=out_shape,
        in_specs=in_specs or [VMEM] * len(operands),
        out_specs=kw.pop("out_specs", (VMEM,) * len(out_shape) if many else VMEM),
        scratch_shapes=list(scratch),
        compiler_params=pltpu.CompilerParams(vmem_limit_bytes=limit * MIB),
        cost_estimate=pl.CostEstimate(flops=flops, bytes_accessed=moved, transcendentals=0),
        **kw,
    )(*operands)


def load_each(refs, at, step):
    out = []
    for ref, n in refs:
        out += [ref[pl.ds(at * n + v, step, stride=n), :] for v in range(n)]
    return out


def pack_kernel(parts, blocks, x_ref, *o_refs):
    width = o_refs[0].shape[-1]

    @pl.loop(0, blocks, unroll=8)
    def _(b):
        x = x_ref[:, pl.ds(pl.multiple_of(b * width, width), width)]
        first = 0
        for ref, n in zip(o_refs, parts):
            ref[pl.ds(b * n, n), :] = x[first : first + n]
            first += n


def inner_kernel(parts, *refs):
    xs, (d_ref, o_ref) = list(zip(refs, parts)), refs[len(parts) :]
    vectors = sum(parts)
    blocks, width = d_ref.shape
    both = pairs(vectors)
    zero = jnp.zeros((8, width), F32)

    def step(c, sums):
        at = pl.multiple_of(c * 8, 8)
        d = d_ref[pl.ds(at, 8), :]
        x = load_each(xs, at, 8)
        y = [a * d for a in x]
        first = [s + x[i] * x[j] for s, (i, j) in zip(sums, both)]
        second = [s + x[i] * y[j] for s, (i, j) in zip(sums[len(both) :], both)]
        return tuple(first + second)

    sums = lax.fori_loop(0, blocks // 8, step, (zero,) * (2 * len(both)))
    for k, s in enumerate(sums):
        o_ref[pl.ds(8 * k, 8), :] = s


def pick_kernel(vectors, slots, where_ref, at_ref, *refs):
    pieces, outs = refs[:-2], refs[-2:]
    for which, out in enumerate(outs):

        @pl.loop(0, slots, unroll=4)
        def _(t):
            m = where_ref[which, t]
            at = at_ref[which, t]
            value = jnp.zeros((vectors, out.shape[-1]), F32)
            for k, piece in enumerate(pieces):
                value = jnp.where(m == k, piece[pl.ds(at, vectors), :], value)
            out[pl.ds(t * vectors, vectors), :] = value


def split(x):
    hi = x.astype(BF16)
    return hi, (x - hi.astype(F32)).astype(BF16)


def multiply_kernel(parts, step, transposed, x_refs, t_ref, o_ref):
    base = pl.program_id(0) * step
    width = o_ref.shape[-1]
    vectors = sum(parts)
    dims = (((1,), (1 if transposed else 0,)), ((), ()))

    def left(t):
        x = [ref[pl.ds(t * n, n), :] for ref, n in zip(x_refs, parts)]
        x = jnp.concatenate(x + [jnp.zeros((8 - vectors, width), F32)], axis=0)
        hi = x.astype(BF16).astype(F32)
        lo = x - hi
        top = jnp.concatenate([hi, hi], axis=1)
        low = jnp.concatenate([lo, jnp.zeros_like(lo)], axis=1)
        return [top, low]

    @pl.loop(0, step // 2)
    def _(p):
        i = 2 * p
        x = jnp.concatenate(left(base + i) + left(base + i + 1), axis=0).astype(BF16)
        along, across = (1, 0) if transposed else (0, 1)
        t = [jnp.concatenate(split(t_ref[i + k]), axis=along) for k in (0, 1)]
        y = lax.dot_general(x, jnp.concatenate(t, axis=across), dims, preferred_element_type=F32)
        o_ref[pl.ds((base + i) * vectors, vectors), :] = (y[0:8, :width] + y[8:16, :width])[:vectors]
        o_ref[pl.ds((base + i + 1) * vectors, vectors), :] = (y[16:24, width:] + y[24:32, width:])[:vectors]


def multiply(xs, tiles, ids, parts, transposed):
    slots, width, _ = tiles.shape
    step = max(s for s in (2, 4, 8, 16, 20) if slots % s == 0)
    rows = sum(parts) * slots
    spec = pl.BlockSpec((step, width, width), lambda i: (i, 0, 0))

    def kernel(*refs):
        x_refs, (t_ref, ids_ref, o_ref) = refs[: len(parts)], refs[len(parts) :]
        multiply_kernel(parts, step, transposed, x_refs, t_ref, o_ref)
        o_ref[pl.ds(rows, 8), :] = ids_ref[...]

    return call(
        kernel, jax.ShapeDtypeStruct((rows + 8, width), F32), (*xs, tiles, ids),
        [VMEM] * len(parts) + [spec, VMEM], 12, flops=slots * 2 * 32 * 256 * 128, grid=(slots // step,), out_specs=VMEM,
    )


def couple_kernel(parts, slots, *refs):
    xs, (y_ref, p_ref, o_ref) = list(zip(refs, parts)), refs[len(parts) :]
    vectors = sum(parts)
    both = pairs(vectors)
    n = len(both)

    def step(c, sums):
        at = pl.multiple_of(8 * c, 8)
        x = load_each(xs, at, 8)
        y = load_each([(y_ref, vectors)], at, 8)
        return tuple(s + (x[i] * y[j] + x[j] * y[i]) for s, (i, j) in zip(sums, both))

    sums = tuple(p_ref[pl.ds(8 * (n + k), 8), :] for k in range(n))
    sums = list(lax.fori_loop(0, slots // 8, step, sums))
    sums = [p_ref[pl.ds(8 * k, 8), :] for k in range(n)] + sums
    for k, s in enumerate(sums):
        o_ref[k : k + 1, :] = jnp.sum(s, axis=0, keepdims=True)
    if o_ref.shape[0] > 2 * n:
        o_ref[2 * n :, :] = jnp.zeros((o_ref.shape[0] - 2 * n, o_ref.shape[1]), F32)
    total = jnp.sum(o_ref[...], axis=1, keepdims=True)
    o_ref[...] = jnp.broadcast_to(total, o_ref.shape)


def add_kernel(vectors, slots, blocks, started, me_ref, *refs):
    o_ref, hot_ref = refs[-2:]
    lists = refs[:-2]
    if started:
        before, lists = lists[0], lists[1:]
    width = o_ref.shape[-1]
    row = lax.broadcasted_iota(jnp.int32, (blocks, width), 0) + me_ref[0] * blocks
    row = row.astype(F32)
    for k, ref in enumerate(lists):
        ids = ref[vectors * slots : vectors * slots + 1, :]
        hot_ref[:, k * width : (k + 1) * width] = jnp.where(ids == row, 1.0, 0.0).astype(BF16)
    group = 2 if vectors % 2 == 0 else 1
    pad = jnp.zeros((width - slots, group * width), F32)

    @pl.loop(0, vectors // group)
    def _(g):
        sums = None
        for k in range(0, len(lists), 2):
            parts = []
            for ref in lists[k : k + 2]:
                y = [ref[pl.ds(g * group + v, slots, stride=vectors), :] for v in range(group)]
                parts += [jnp.concatenate(y, axis=1), pad]
            y = jnp.concatenate(parts, axis=0)
            hi = y.astype(BF16)
            lo = (y - hi.astype(F32)).astype(BF16)
            hot = hot_ref[:, k * width : (k + 2) * width]
            part = jnp.dot(hot, hi, preferred_element_type=F32) + jnp.dot(hot, lo, preferred_element_type=F32)
            sums = part if sums is None else sums + part
        for v in range(group):
            at = pl.multiple_of((g * group + v) * blocks, 8)
            s = sums[:, v * width : (v + 1) * width]
            if started:
                s = s + before[pl.ds(at, blocks), :]
            o_ref[pl.ds(at, blocks), :] = s


def add_lists(me, lists, vectors, slots, blocks, before=None):
    width = lists[0].shape[-1]
    operands = (me,) + (() if before is None else (before,)) + tuple(lists)
    return call(
        functools.partial(add_kernel, vectors, slots, blocks, before is not None),
        jax.ShapeDtypeStruct((vectors * blocks, width), F32), operands,
        [SMEM] + [VMEM] * (len(operands) - 1), 16,
        scratch=(pltpu.VMEM((blocks, len(lists) * width), BF16),), flops=len(lists) * 2 * 256 * 256 * 768,
    )


def algebra(vectors, total, sums_ref):
    both = pairs(vectors)
    n = len(both)
    g, q = {}, {}
    for k, (i, j) in enumerate(both):
        g[i, j] = sums_ref[k : k + 1, :] * (1.0 / total)
        q[i, j] = q[j, i] = sums_ref[n + k : n + k + 1, :] * (1.0 / total)
    low, inv = {}, {}
    rev = []
    for j in range(vectors):
        s = g[j, j]
        for k in range(j):
            s = s - low[j, k] * low[j, k]
        rev.append(1.0 / jnp.sqrt(s))
        for i in range(j + 1, vectors):
            s = g[i, j]
            for k in range(j):
                s = s - low[i, k] * low[j, k]
            low[i, j] = s * rev[j]
    for j in range(vectors):
        inv[j, j] = rev[j]
        for i in range(j + 1, vectors):
            s = low[i, j] * inv[j, j]
            for k in range(j + 1, i):
                s = s + low[i, k] * inv[k, j]
            inv[i, j] = -s * rev[i]
    half, onto, proj = {}, {}, {}
    for i in range(vectors):
        for j in range(vectors):
            half[i, j] = sum(inv[i, k] * q[k, j] for k in range(i + 1))
    for i in range(vectors):
        for j in range(vectors):
            proj[i, j] = sum(half[i, k] * inv[j, k] for k in range(j + 1))
    for i in range(vectors):
        for j in range(vectors):
            onto[i, j] = sum(proj[i, k] * inv[k, j] for k in range(j, vectors))
    return inv, onto


def finish_kernel(parts, total, sums_ref, *refs):
    xs, (d_ref, m_ref, final_ref, residual_ref, coef, res, fin) = list(zip(refs, parts)), refs[len(parts) :]
    vectors = sum(parts)
    blocks, width = d_ref.shape
    inv, onto = algebra(vectors, total, sums_ref)
    places = {}
    for name, table in (("i", inv), ("o", onto)):
        for key in sorted(table):
            k = len(places)
            places[name, key] = k
            coef[pl.ds(8 * k, 8), :] = jnp.broadcast_to(table[key], (8, width))

    @pl.loop(0, blocks // 8, unroll=2)
    def _(c):
        at = pl.multiple_of(c * 8, 8)
        d = d_ref[pl.ds(at, 8), :]
        rd = 1.0 / d
        x = load_each(xs, at, 8)
        m = [m_ref[pl.ds(v * blocks + at, 8), :] + x[v] * d for v in range(vectors)]

        def value(name, i, j):
            return coef[pl.ds(8 * places[name, (i, j)], 8), :]

        for i in range(vectors):
            basis = r = None
            for j in range(i + 1):
                f = value("i", i, j)
                basis = f * x[j] if basis is None else basis + f * x[j]
                r = f * m[j] if r is None else r + f * m[j]
            for j in range(vectors):
                r = r - value("o", i, j) * x[j]
            res[pl.ds(8 * at + i, 8, stride=8), :] = r
            fin[pl.ds(8 * at + i, 8, stride=8), :] = basis - r * rd

    @pl.loop(0, blocks, unroll=8)
    def _(b):
        at = pl.multiple_of(b * width, width)
        residual_ref[:, pl.ds(at, width)] = res[pl.ds(pl.multiple_of(8 * b, 8), vectors), :]
        final_ref[:, pl.ds(at, width)] = fin[pl.ds(pl.multiple_of(8 * b, 8), vectors), :]


def body(start_block, diagonal, tile_values, tile_rows, tile_cols, tile_counts, offset_map):
    tiles = tile_values[0, 0]
    live_count = tile_counts[0, 0]
    row_size = lax.axis_size("row")
    off_size = lax.axis_size("off")
    me = lax.axis_index("off").astype(jnp.int32)
    vectors, shard = start_block.shape
    slots, width, _ = tiles.shape
    blocks = shard // width
    total = shard * off_size * row_size
    count = len(pairs(vectors))
    parts = [vectors - vectors // 2, vectors // 2]
    row_bits, off_bits = bits_of("row")[::-1], bits_of("off")

    packed = call(
        functools.partial(pack_kernel, parts, blocks),
        tuple(jax.ShapeDtypeStruct((n * blocks, width), F32) for n in parts), (start_block,),
    )
    live = jnp.arange(slots, dtype=jnp.int32) < live_count
    row_ids = jnp.where(live, tile_rows[0, 0], -1)
    col_ids = jnp.where(live, tile_cols[0, 0], -1)

    def padded(ids):
        return jnp.pad(ids.astype(F32)[None, :], ((0, 7), (0, width - slots)), constant_values=-1)

    diagonal = diagonal.reshape(blocks, width)

    arrangements = list(itertools.permutations(range(off_size))) if off_size <= 4 else []
    listed = off_size == row_size // 2 and arrangements
    if listed:
        matches = jnp.all(jnp.array(arrangements, jnp.int32) == offset_map[None, :], axis=1)
        which = jnp.argmax(matches).astype(jnp.int32)

    def routed(function, *operands):
        if listed:

            def branch(distances):
                return functools.partial(function, lambda x, sign: shift(x, [sign * d for d in distances]))

            return lax.switch(which, [branch(a) for a in arrangements], *operands)

        def move(x, sign):
            for b in range((row_size // 2).bit_length() - 1):
                moved = shift(x, [sign << b] * off_size)
                x = jnp.where(offset_map[me] >> b & 1 == 1, moved, x)
            return x

        return function(move, *operands)

    row_line, col_line = padded(row_ids), padded(col_ids)
    group_line = routed(lambda move, x: move(x, 1), col_line)
    both = jnp.stack([row_ids, group_line[0, :slots].astype(jnp.int32)])
    where = jnp.where(both < 0, -1, (both // blocks) ^ me)
    at = jnp.where(both < 0, 0, both % blocks)

    def pick(k, hold):
        n = parts[k]
        pieces = gather_off({0: packed[k]}, off_bits, hold)
        picked = jax.ShapeDtypeStruct((n * slots, width), F32)
        return call(
            functools.partial(pick_kernel, n, slots), (picked, picked),
            (where, at * n, *pieces), [SMEM, SMEM] + [VMEM] * off_size,
        )

    inner = call(
        functools.partial(inner_kernel, parts),
        jax.ShapeDtypeStruct((16 * count, width), F32), (*packed, diagonal),
    )
    row0, col0 = pick(0, (where, at, inner))
    arrived0 = routed(lambda move, x: move(x, -1), col0)
    row1, col1 = pick(1, (arrived0,))

    def run(move, rows, arrived0, col1, inner, tiles, row_line, col_line):
        arrived = [arrived0, move(col1, -1)]
        mirrored = multiply(rows, tiles, col_line, parts, False)
        returned = move(mirrored, 1)
        direct = multiply(arrived, tiles, row_line, parts, True)
        sums = call(
            functools.partial(couple_kernel, parts, slots),
            jax.ShapeDtypeStruct((-(-2 * count // 8) * 8, width), F32), (*rows, direct, inner),
        )
        stages = [sums]
        for axis, bit in [("off", off_bits[0])] + [("row", b) for b in row_bits[:-1]]:
            stages.append(sum_step(stages[-1], axis, bit))
        direct_over = swap(after(direct, stages[0]), "off", off_bits[0])
        returned_over = swap(after(returned, stages[1]), "off", off_bits[0])
        return stages[-1], direct, direct_over, returned, returned_over

    done = routed(run, [row0, row1], arrived0, col1, inner, tiles, row_line, col_line)
    sums, direct, direct_over, returned, returned_over = done
    top = off_bits[0]
    sums = sum_step(sums, "row", row_bits[-1])
    direct = gather_off({0: direct, top: direct_over}, off_bits[1:])
    returned = gather_off({0: returned, top: returned_over}, off_bits[1:])
    lists = [y for pair in zip(direct, returned) for y in pair]
    image = add_lists(me[None], lists[:off_size], vectors, slots, blocks)
    image = add_lists(me[None], lists[off_size:], vectors, slots, blocks, image)
    sums = after(sums, image)
    for bit in off_bits[1:]:
        sums = sum_step(sums, "off", bit)
    out = jax.ShapeDtypeStruct((vectors, shard), F32)
    return call(
        functools.partial(finish_kernel, parts, float(total)), (out, out),
        (sums, *packed, diagonal, image), limit=24,
        scratch=(
            pltpu.VMEM((8 * (vectors * vectors + count), width), F32),
            pltpu.VMEM((8 * blocks, width), F32),
            pltpu.VMEM((8 * blocks, width), F32),
        ),
    )


def solution(mesh):
    return jax.shard_map(
        body,
        mesh=mesh,
        in_specs=(
            P(None, ("row", "off")),
            P(("row", "off")),
            P("row", "off", None, None, None),
            P("row", "off", None),
            P("row", "off", None),
            P("row", "off"),
            P(),
        ),
        out_specs=(P(None, ("row", "off")), P(None, ("row", "off"))),
        check_vma=False,
    )
```

profile of v0, /device:TPU:0, one launch (start us, length us, event | category | flops | bytes accessed | tf_op | source)
XLA Modules:
  0.0 106.3 jit_solution(2494898363025183356)
XLA Ops:
  0.6 1.2 %copy-done = f32[6,32768]{1,0:T(8,128)S(1)} copy-done((f32[6,32768]{1,0:T(8,128)S(1)}, f32[6,32768]{1,0:T(8,128)}, u32[]{:S(2)}) %copy-start) | copy-done | bytes 786456
  2.3 3.1 %collective-permute-start.219 = (f32[768,128]{1,0:T(8,128)S(1)}, f32[768,128]{1,0:T(8,128)S(1)}, u32[]{:S(2)}, u32[]{:S(2)}) collective-permute-start(f32[768,128]{1,0:T(8,128)S(1)} %get-tuple-element.750.refs_0_), channel_id=1, source_target_pairs={{0,2},{1,3},{2,0},{3,1},{4,6},{5,7},{6,4},{7,5},{8,10},{9,11},{10,... | collective-permute-start | bytes 1179656 | tf_op jit(solution)/shard_map/ppermute | solution.py:21
  9.4 8.3 %conditional.3 = (f32[8,128]{1,0:T(8,128)}) conditional(s32[]{:T(128)} %clamp.2, f32[8,128]{1,0:T(8,128)S(1)} %pad.9, f32[8,128]{1,0:T(8,128)S(1)} %pad.9, f32[8,128]{1,0:T(8,128)S(1)} %pad.9, f32[8,128]{1,0:T(8,128)S(1)} %pad.9, f32[8,128]{1,0:T(8,128)S(1)} %pad.9, f32[8,128]{1,0:T(8,128)S(1)} %pad.9, ...), branch_computations={%region_2.3_spmd, %region_3.4_spmd, %region_4.5_spmd, %region_5.6_... | conditional | bytes 16432 | solution.py:365
  9.5 3.4 %collective-permute-start.8 = (f32[8,128]{1,0:T(8,128)S(1)}, f32[8,128]{1,0:T(8,128)}, u32[]{:S(2)}, u32[]{:S(2)}) collective-permute-start(f32[8,128]{1,0:T(8,128)S(1)} %param.8), channel_id=1, source_target_pairs={{0,4},{1,9},{2,2},{3,15},{4,8},{5,13},{6,6},{7,19},{8,12},{9,17},{... | collective-permute-start | bytes 12296 | tf_op jit(solution)/shard_map/cond/branch_8_fun/ppermute | solution.py:31
  12.9 4.9 %collective-permute-done.8 = f32[8,128]{1,0:T(8,128)} collective-permute-done((f32[8,128]{1,0:T(8,128)S(1)}, f32[8,128]{1,0:T(8,128)}, u32[]{:S(2)}, u32[]{:S(2)}) %collective-permute-start.8) | collective-permute-done | bytes 4128 | tf_op jit(solution)/shard_map/cond/branch_8_fun/ppermute | solution.py:31
  20.7 1.2 %collective-permute-done.220.refs_3_ = f32[768,128]{1,0:T(8,128)S(1)} collective-permute-done((f32[768,128]{1,0:T(8,128)S(1)}, f32[768,128]{1,0:T(8,128)S(1)}, u32[]{:S(2)}, u32[]{:S(2)}) %collective-permute-start.220) | collective-permute-done | bytes 393248 | tf_op jit(solution)/shard_map/ppermute | solution.py:21
  22.0 1.7 %shard_map.97 = (f32[240,128]{1,0:T(8,128)S(1)}, f32[240,128]{1,0:T(8,128)S(1)}) custom-call(s32[2,80]{1,0:T(2,128)S(1)} %get-tuple-element.768.where_ref, s32[2,80]{1,0:T(2,128)S(1)} %get-tuple-element.766.at_ref, f32[768,128]{1,0:T(8,128)S(1)} %get-tuple-element.750.refs_0_, f32[768,128]{1,0:T(8,128)S(1)} %collective-permute-done.218.refs_1_, ...), custom_call_target="tpu_custom_call" | custom-call | bytes 1574144 | tf_op jit(solution)/shard_map/pallas_call | solution.py:62
  23.6 8.1 %conditional.4 = (f32[240,128]{1,0:T(8,128)}) conditional(s32[]{:T(128)} %clamp.2, f32[240,128]{1,0:T(8,128)S(1)} %get-tuple-element.752, f32[240,128]{1,0:T(8,128)S(1)} %get-tuple-element.752, f32[240,128]{1,0:T(8,128)S(1)} %get-tuple-element.752, f32[240,128]{1,0:T(8,128)S(1)} %get-tuple-element.752, ...), branch_computations={%region_26.27_spmd, %region_27.28_spmd, %region_28.29_spmd, %regio... | conditional | bytes 491568 | solution.py:365
  23.7 3.2 %collective-permute-start.32 = (f32[240,128]{1,0:T(8,128)S(1)}, f32[240,128]{1,0:T(8,128)}, u32[]{:S(2)}, u32[]{:S(2)}) collective-permute-start(f32[240,128]{1,0:T(8,128)S(1)} %param.32), channel_id=1, source_target_pairs={{0,28},{1,25},{2,2},{3,23},{4,0},{5,29},{6,6},{7,27},{8,4},{9,1},{... | collective-permute-start | bytes 368648 | tf_op jit(solution)/shard_map/cond/branch_8_fun/ppermute | solution.py:31
  26.9 4.8 %collective-permute-done.32 = f32[240,128]{1,0:T(8,128)} collective-permute-done((f32[240,128]{1,0:T(8,128)S(1)}, f32[240,128]{1,0:T(8,128)}, u32[]{:S(2)}, u32[]{:S(2)}) %collective-permute-start.32) | collective-permute-done | bytes 122912 | tf_op jit(solution)/shard_map/cond/branch_8_fun/ppermute | solution.py:31
  31.9 1.6 %collective-permute-done.221.refs_3_ = f32[768,128]{1,0:T(8,128)S(1)} collective-permute-done((f32[768,128]{1,0:T(8,128)S(1)}, f32[768,128]{1,0:T(8,128)S(1)}, u32[]{:S(2)}, u32[]{:S(2)}) %collective-permute-start.221) | collective-permute-done | bytes 393248 | tf_op jit(solution)/shard_map/ppermute | solution.py:21
  33.5 1.7 %shard_map.98 = (f32[240,128]{1,0:T(8,128)S(1)}, f32[240,128]{1,0:T(8,128)S(1)}) custom-call(s32[2,80]{1,0:T(2,128)S(1)} %get-tuple-element.768.where_ref, s32[2,80]{1,0:T(2,128)S(1)} %get-tuple-element.766.at_ref, f32[768,128]{1,0:T(8,128)S(1)} %get-tuple-element.749.refs_1_.refs_0_, f32[768,128]{1,0:T(8,128)S(1)} %collective-permute-done.216.refs_1_, ...), custom_call_target="tpu_custom_call" | custom-call | bytes 1574144 | tf_op jit(solution)/shard_map/pallas_call | solution.py:62
  35.2 47.4 %conditional.5 = (f32[488,128]{1,0:T(8,128)}, f32[488,128]{1,0:T(8,128)S(1)}, f32[488,128]{1,0:T(8,128)}, f32[488,128]{1,0:T(8,128)}, f32[488,128]{1,0:T(8,128)}...) conditional(s32[]{:T(128)} %clamp.2, ...), branch_computations={%region_50.51_spmd, %region_51.52_spmd, %region_52.53_spmd, %regio... | conditional | flops 335556608 | bytes 37106036 | solution.py:365
  35.3 7.6 %branch_8_fun.5 = f32[488,128]{1,0:T(8,128)S(1)} custom-call(f32[240,128]{1,0:T(8,128)S(1)} %get-tuple-element.574.refs_0_, f32[240,128]{1,0:T(8,128)S(1)} %get-tuple-element.575.refs_1_, f32[80,128,128]{2,1,0:T(8,128)} %get-tuple-element.572.refs_2_, f32[8,128]{1,0:T(8,128)S(1)} %get-tuple-element.578.refs_3_), custom_call_target="tpu_custom_call" | custom-call | flops 167772160 | bytes 5492736 | tf_op jit(solution)/shard_map/cond/branch_8_fun/pallas_call | solution.py:62
  42.9 4.1 %collective-permute-start.106 = (f32[488,128]{1,0:T(8,128)S(1)}, f32[488,128]{1,0:T(8,128)}, u32[]{:S(2)}, u32[]{:S(2)}) collective-permute-start(f32[488,128]{1,0:T(8,128)S(1)} %branch_8_fun.5), channel_id=1, source_target_pairs={{0,4},{1,9},{2,2},{3,15},{4,8},{5,13},{6,6},{7,19},{8,12},{9,17},{... | collective-permute-start | bytes 749576 | tf_op jit(solution)/shard_map/cond/branch_8_fun/ppermute | solution.py:31
  47.0 5.6 %collective-permute-start.104 = (f32[240,128]{1,0:T(8,128)S(1)}, f32[240,128]{1,0:T(8,128)S(1)}, u32[]{:S(2)}, u32[]{:S(2)}) collective-permute-start(f32[240,128]{1,0:T(8,128)S(1)} %get-tuple-element.571), channel_id=1, source_target_pairs={{0,28},{1,25},{2,2},{3,23},{4,0},{5,29},{6,6},{7,27},{8,4},{9,1},{... | collective-permute-start | bytes 368648 | tf_op jit(solution)/shard_map/cond/branch_8_fun/ppermute | solution.py:31
  52.7 4.9 %collective-permute-done.104.refs_1_ = f32[240,128]{1,0:T(8,128)S(1)} collective-permute-done((f32[240,128]{1,0:T(8,128)S(1)}, f32[240,128]{1,0:T(8,128)S(1)}, u32[]{:S(2)}, u32[]{:S(2)}) %collective-permute-start.104) | collective-permute-done | bytes 122912 | tf_op jit(solution)/shard_map/cond/branch_8_fun/ppermute | solution.py:31
  57.6 9.2 %branch_8_fun.3.refs_2_ = f32[488,128]{1,0:T(8,128)} custom-call(f32[240,128]{1,0:T(8,128)} %get-tuple-element.570.refs_0_, f32[240,128]{1,0:T(8,128)S(1)} %collective-permute-done.104.refs_1_, f32[80,128,128]{2,1,0:T(8,128)S(1)} %copy-done.11, f32[8,128]{1,0:T(8,128)S(1)} %get-tuple-element.573.refs_3_), custom_call_target="tpu_custom_call" | custom-call | flops 167772160 | bytes 5492736 | tf_op jit(solution)/shard_map/cond/branch_8_fun/pallas_call | solution.py:62
  66.8 1.3 %branch_8_fun.4 = f32[48,128]{1,0:T(8,128)S(1)} custom-call(f32[240,128]{1,0:T(8,128)S(1)} %get-tuple-element.574.refs_0_, f32[240,128]{1,0:T(8,128)S(1)} %get-tuple-element.575.refs_1_, f32[488,128]{1,0:T(8,128)} %branch_8_fun.3.refs_2_, f32[336,128]{1,0:T(8,128)S(1)} %get-tuple-element.576.refs_3_), custom_call_target="tpu_custom_call" | custom-call | bytes 667648 | tf_op jit(solution)/shard_map/cond/branch_8_fun/pallas_call | solution.py:62
  68.0 2.0 %collective-permute-start.105 = (f32[488,128]{1,0:T(8,128)}, f32[488,128]{1,0:T(8,128)}, u32[]{:S(2)}, u32[]{:S(2)}) collective-permute-start(f32[488,128]{1,0:T(8,128)} %branch_8_fun.3.refs_2_), channel_id=1, source_target_pairs={{0,2},{1,3},{2,0},{3,1},{4,6},{5,7},{6,4},{7,5},{8,10},{9,11},{10,... | collective-permute-start | bytes 749576 | tf_op jit(solution)/shard_map/cond/branch_8_fun/ppermute | solution.py:21
  70.0 1.8 %collective-permute-done.107 = f32[48,128]{1,0:T(8,128)S(1)} collective-permute-done((f32[48,128]{1,0:T(8,128)S(1)}, f32[48,128]{1,0:T(8,128)S(1)}, u32[]{:S(2)}, u32[]{:S(2)}) %collective-permute-start.107) | collective-permute-done | bytes 24608 | tf_op jit(solution)/shard_map/cond/branch_8_fun/ppermute | solution.py:21
  71.9 2.1 %collective-permute-start.109 = (f32[48,128]{1,0:T(8,128)S(1)}, f32[48,128]{1,0:T(8,128)S(1)}, u32[]{:S(2)}, u32[]{:S(2)}) collective-permute-start(f32[48,128]{1,0:T(8,128)S(1)} %add.143), channel_id=1, source_target_pairs={{0,4},{4,0},{8,12},{12,8},{16,20},{20,16},{24,28},{28,24},{1,5},{5... | collective-permute-start | bytes 73736 | tf_op jit(solution)/shard_map/cond/branch_8_fun/ppermute | solution.py:21
  74.0 2.1 %collective-permute-done.109 = f32[48,128]{1,0:T(8,128)S(1)} collective-permute-done((f32[48,128]{1,0:T(8,128)S(1)}, f32[48,128]{1,0:T(8,128)S(1)}, u32[]{:S(2)}, u32[]{:S(2)}) %collective-permute-start.109) | collective-permute-done | bytes 24608 | tf_op jit(solution)/shard_map/cond/branch_8_fun/ppermute | solution.py:21
  76.7 1.4 %collective-permute-start.110 = (f32[48,128]{1,0:T(8,128)}, f32[48,128]{1,0:T(8,128)}, u32[]{:S(2)}, u32[]{:S(2)}) collective-permute-start(f32[48,128]{1,0:T(8,128)} %add.144), channel_id=1, source_target_pairs={{0,8},{4,12},{8,0},{12,4},{16,24},{20,28},{24,16},{28,20},{1,9},{5... | collective-permute-start | bytes 73736 | tf_op jit(solution)/shard_map/cond/branch_8_fun/ppermute | solution.py:21
  80.9 1.7 %collective-permute-done.108 = f32[488,128]{1,0:T(8,128)} collective-permute-done((f32[488,128]{1,0:T(8,128)}, f32[488,128]{1,0:T(8,128)}, u32[]{:S(2)}, u32[]{:S(2)}) %collective-permute-start.108) | collective-permute-done | bytes 249888 | tf_op jit(solution)/shard_map/cond/branch_8_fun/ppermute | solution.py:21
  83.2 3.8 %collective-permute-start.226 = (f32[488,128]{1,0:T(8,128)}, f32[488,128]{1,0:T(8,128)S(1)}, u32[]{:S(2)}, u32[]{:S(2)}) collective-permute-start(f32[488,128]{1,0:T(8,128)} %get-tuple-element.762.refs_2_), channel_id=1, source_target_pairs={{0,1},{1,0},{2,3},{3,2},{4,5},{5,4},{6,7},{7,6},{8,9},{9,8},{10,11... | collective-permute-start | bytes 749576 | tf_op jit(solution)/shard_map/ppermute | solution.py:21
  87.8 5.7 %collective-permute-start.222 = (f32[48,128]{1,0:T(8,128)S(1)}, f32[48,128]{1,0:T(8,128)S(1)}, u32[]{:S(2)}, u32[]{:S(2)}) collective-permute-start(f32[48,128]{1,0:T(8,128)S(1)} %add.189), channel_id=1, source_target_pairs={{0,16},{4,20},{8,24},{12,28},{16,0},{20,4},{24,8},{28,12},{1,17},{... | collective-permute-start | bytes 73736 | tf_op jit(solution)/shard_map/ppermute | solution.py:21
  93.5 4.6 %collective-permute-done.222 = f32[48,128]{1,0:T(8,128)S(1)} collective-permute-done((f32[48,128]{1,0:T(8,128)S(1)}, f32[48,128]{1,0:T(8,128)S(1)}, u32[]{:S(2)}, u32[]{:S(2)}) %collective-permute-start.222) | collective-permute-done | bytes 24608 | tf_op jit(solution)/shard_map/ppermute | solution.py:21
  98.1 1.9 %shard_map.99.refs_0_ = f32[1536,128]{1,0:T(8,128)S(1)} custom-call(s32[1]{0:T(128)} %bitcast.5.me_ref, f32[488,128]{1,0:T(8,128)S(1)} %get-tuple-element.759.refs_0_, f32[488,128]{1,0:T(8,128)} %get-tuple-element.760.refs_1_, f32[488,128]{1,0:T(8,128)S(1)} %collective-permute-done.223.refs_2_, f32[488,128]{1,0:T(8,128)S(1)} %collective-permute-done.224.refs_3_), custom_call_target="tpu_custom_call" | custom-call | flops 402653184 | bytes 999428 | tf_op jit(solution)/shard_map/pallas_call | solution.py:62
  100.1 2.0 %shard_map.100.refs_3_ = f32[1536,128]{1,0:T(8,128)S(1)} custom-call(s32[1]{0:T(128)} %bitcast.5.me_ref, f32[1536,128]{1,0:T(8,128)S(1)} %shard_map.99.refs_0_, f32[488,128]{1,0:T(8,128)} %get-tuple-element.761.refs_1_, f32[488,128]{1,0:T(8,128)} %get-tuple-element.762.refs_2_, f32[488,128]{1,0:T(8,128)S(1)} %collective-permute-done.225.refs_3_, ...), custom_call_target="tpu_custom_call" | custom-call | flops 402653184 | bytes 1785860 | tf_op jit(solution)/shard_map/pallas_call | solution.py:62
  102.2 1.2 %collective-permute-done.227 = f32[48,128]{1,0:T(8,128)S(1)} collective-permute-done((f32[48,128]{1,0:T(8,128)S(1)}, f32[48,128]{1,0:T(8,128)S(1)}, u32[]{:S(2)}, u32[]{:S(2)}) %collective-permute-start.227) | collective-permute-done | bytes 24608 | tf_op jit(solution)/shard_map/ppermute | solution.py:21
  103.4 2.9 %shard_map.101 = (f32[6,32768]{1,0:T(8,128)}, f32[6,32768]{1,0:T(8,128)}) custom-call(f32[48,128]{1,0:T(8,128)S(1)} %add.191.sums_ref, f32[768,128]{1,0:T(8,128)S(1)} %get-tuple-element.750.refs_0_, f32[768,128]{1,0:T(8,128)S(1)} %get-tuple-element.749.refs_1_.refs_0_, f32[256,128]{1,0:T(8,128)S(1)} %bitcast.12, f32[1536,128]{1,0:T(8,128)S(1)} %shard_map.100.refs_3_), custom_call_target="tpu_custom_call" | custom-call | bytes 1728512 | tf_op jit(solution)/shard_map/pallas_call | solution.py:62
  (46 shorter events, 11.1 us)
Async XLA Ops:
  0.6 1.2 %copy-start = (f32[6,32768]{1,0:T(8,128)S(1)}, f32[6,32768]{1,0:T(8,128)}, u32[]{:S(2)}) copy-start(f32[6,32768]{1,0:T(8,128)} %x_ref.1) | copy-start | bytes 2359300
  2.3 17.8 %collective-permute-start.219 = (f32[768,128]{1,0:T(8,128)S(1)}, f32[768,128]{1,0:T(8,128)S(1)}, u32[]{:S(2)}, u32[]{:S(2)}) collective-permute-start(f32[768,128]{1,0:T(8,128)S(1)} %get-tuple-element.750.refs_0_), channel_id=1, source_target_pairs={{0,2},{1,3},{2,0},{3,1},{4,6},{5,7},{6,4},{7,5},{8,10},{9,11},{10,... | collective-permute-start | bytes 1179656 | tf_op jit(solution)/shard_map/ppermute | solution.py:21
  5.4 15.4 %collective-permute-start.218 = (f32[768,128]{1,0:T(8,128)S(1)}, f32[768,128]{1,0:T(8,128)S(1)}, u32[]{:S(2)}, u32[]{:S(2)}) collective-permute-start(f32[768,128]{1,0:T(8,128)S(1)} %get-tuple-element.750.refs_0_), channel_id=1, source_target_pairs={{0,1},{1,0},{2,3},{3,2},{4,5},{5,4},{6,7},{7,6},{8,9},{9,8},{10,11... | collective-permute-start | bytes 1179656 | tf_op jit(solution)/shard_map/ppermute | solution.py:21
  9.5 8.3 %collective-permute-start.8 = (f32[8,128]{1,0:T(8,128)S(1)}, f32[8,128]{1,0:T(8,128)}, u32[]{:S(2)}, u32[]{:S(2)}) collective-permute-start(f32[8,128]{1,0:T(8,128)S(1)} %param.8), channel_id=1, source_target_pairs={{0,4},{1,9},{2,2},{3,15},{4,8},{5,13},{6,6},{7,19},{8,12},{9,17},{... | collective-permute-start | bytes 12296 | tf_op jit(solution)/shard_map/cond/branch_8_fun/ppermute | solution.py:31
  17.8 0.9 copy-start.1
  20.2 1.8 %collective-permute-start.220 = (f32[768,128]{1,0:T(8,128)S(1)}, f32[768,128]{1,0:T(8,128)S(1)}, u32[]{:S(2)}, u32[]{:S(2)}) collective-permute-start(f32[768,128]{1,0:T(8,128)S(1)} %collective-permute-done.219.refs_2_), channel_id=1, source_target_pairs={{0,1},{1,0},{2,3},{3,2},{4,5},{5,4},{6,7},{7,6},{8,9},{9,8},{10,11... | collective-permute-start | bytes 1179656 | tf_op jit(solution)/shard_map/ppermute | solution.py:21
  20.2 11.5 %collective-permute-start.217 = (f32[768,128]{1,0:T(8,128)S(1)}, f32[768,128]{1,0:T(8,128)S(1)}, u32[]{:S(2)}, u32[]{:S(2)}) collective-permute-start(f32[768,128]{1,0:T(8,128)S(1)} %get-tuple-element.749.refs_1_.refs_0_), channel_id=1, source_target_pairs={{0,2},{1,3},{2,0},{3,1},{4,6},{5,7},{6,4},{7,5},{8,10},{9,11},{10,... | collective-permute-start | bytes 1179656 | tf_op jit(solution)/shard_map/ppermute | solution.py:21
  20.3 11.6 %collective-permute-start.216 = (f32[768,128]{1,0:T(8,128)S(1)}, f32[768,128]{1,0:T(8,128)S(1)}, u32[]{:S(2)}, u32[]{:S(2)}) collective-permute-start(f32[768,128]{1,0:T(8,128)S(1)} %get-tuple-element.749.refs_1_.refs_0_), channel_id=1, source_target_pairs={{0,1},{1,0},{2,3},{3,2},{4,5},{5,4},{6,7},{7,6},{8,9},{9,8},{10,11... | collective-permute-start | bytes 1179656 | tf_op jit(solution)/shard_map/ppermute | solution.py:21
  23.7 8.1 %collective-permute-start.32 = (f32[240,128]{1,0:T(8,128)S(1)}, f32[240,128]{1,0:T(8,128)}, u32[]{:S(2)}, u32[]{:S(2)}) collective-permute-start(f32[240,128]{1,0:T(8,128)S(1)} %param.32), channel_id=1, source_target_pairs={{0,28},{1,25},{2,2},{3,23},{4,0},{5,29},{6,6},{7,27},{8,4},{9,1},{... | collective-permute-start | bytes 368648 | tf_op jit(solution)/shard_map/cond/branch_8_fun/ppermute | solution.py:31
  31.8 1.7 %collective-permute-start.221 = (f32[768,128]{1,0:T(8,128)S(1)}, f32[768,128]{1,0:T(8,128)S(1)}, u32[]{:S(2)}, u32[]{:S(2)}) collective-permute-start(f32[768,128]{1,0:T(8,128)S(1)} %collective-permute-done.217.refs_2_), channel_id=1, source_target_pairs={{0,1},{1,0},{2,3},{3,2},{4,5},{5,4},{6,7},{7,6},{8,9},{9,8},{10,11... | collective-permute-start | bytes 1179656 | tf_op jit(solution)/shard_map/ppermute | solution.py:21
  35.2 68.2 %copy-start.2 = (f32[32768]{0:T(1024)S(1)}, f32[32768]{0:T(1024)}, u32[]{:S(2)}) copy-start(f32[32768]{0:T(1024)} %param.81) | copy-start | bytes 393220
  35.3 22.3 %copy-start.11 = (f32[80,128,128]{2,1,0:T(8,128)S(1)}, f32[80,128,128]{2,1,0:T(8,128)}, u32[]{:S(2)}) copy-start(f32[80,128,128]{2,1,0:T(8,128)} %get-tuple-element.572.refs_2_) | copy-start | bytes 15728644 | tf_op jit(solution)/shard_map/cond
  42.9 29.0 %collective-permute-start.106 = (f32[488,128]{1,0:T(8,128)S(1)}, f32[488,128]{1,0:T(8,128)}, u32[]{:S(2)}, u32[]{:S(2)}) collective-permute-start(f32[488,128]{1,0:T(8,128)S(1)} %branch_8_fun.5), channel_id=1, source_target_pairs={{0,4},{1,9},{2,2},{3,15},{4,8},{5,13},{6,6},{7,19},{8,12},{9,17},{... | collective-permute-start | bytes 749576 | tf_op jit(solution)/shard_map/cond/branch_8_fun/ppermute | solution.py:31
  47.0 10.5 %collective-permute-start.104 = (f32[240,128]{1,0:T(8,128)S(1)}, f32[240,128]{1,0:T(8,128)S(1)}, u32[]{:S(2)}, u32[]{:S(2)}) collective-permute-start(f32[240,128]{1,0:T(8,128)S(1)} %get-tuple-element.571), channel_id=1, source_target_pairs={{0,28},{1,25},{2,2},{3,23},{4,0},{5,29},{6,6},{7,27},{8,4},{9,1},{... | collective-permute-start | bytes 368648 | tf_op jit(solution)/shard_map/cond/branch_8_fun/ppermute | solution.py:31
  68.0 3.8 %collective-permute-start.107 = (f32[48,128]{1,0:T(8,128)S(1)}, f32[48,128]{1,0:T(8,128)S(1)}, u32[]{:S(2)}, u32[]{:S(2)}) collective-permute-start(f32[48,128]{1,0:T(8,128)S(1)} %branch_8_fun.4), channel_id=1, source_target_pairs={{0,2},{1,3},{2,0},{3,1},{4,6},{5,7},{6,4},{7,5},{8,10},{9,11},{10,... | collective-permute-start | bytes 73736 | tf_op jit(solution)/shard_map/cond/branch_8_fun/ppermute | solution.py:21
  68.0 12.8 %collective-permute-start.105 = (f32[488,128]{1,0:T(8,128)}, f32[488,128]{1,0:T(8,128)}, u32[]{:S(2)}, u32[]{:S(2)}) collective-permute-start(f32[488,128]{1,0:T(8,128)} %branch_8_fun.3.refs_2_), channel_id=1, source_target_pairs={{0,2},{1,3},{2,0},{3,1},{4,6},{5,7},{6,4},{7,5},{8,10},{9,11},{10,... | collective-permute-start | bytes 749576 | tf_op jit(solution)/shard_map/cond/branch_8_fun/ppermute | solution.py:21
  71.9 10.7 %collective-permute-start.108 = (f32[488,128]{1,0:T(8,128)}, f32[488,128]{1,0:T(8,128)}, u32[]{:S(2)}, u32[]{:S(2)}) collective-permute-start(f32[488,128]{1,0:T(8,128)} %collective-permute-done.106), channel_id=1, source_target_pairs={{0,2},{1,3},{2,0},{3,1},{4,6},{5,7},{6,4},{7,5},{8,10},{9,11},{10,... | collective-permute-start | bytes 749576 | tf_op jit(solution)/shard_map/cond/branch_8_fun/ppermute | solution.py:21
  71.9 4.2 %collective-permute-start.109 = (f32[48,128]{1,0:T(8,128)S(1)}, f32[48,128]{1,0:T(8,128)S(1)}, u32[]{:S(2)}, u32[]{:S(2)}) collective-permute-start(f32[48,128]{1,0:T(8,128)S(1)} %add.143), channel_id=1, source_target_pairs={{0,4},{4,0},{8,12},{12,8},{16,20},{20,16},{24,28},{28,24},{1,5},{5... | collective-permute-start | bytes 73736 | tf_op jit(solution)/shard_map/cond/branch_8_fun/ppermute | solution.py:21
  76.7 4.1 %collective-permute-start.110 = (f32[48,128]{1,0:T(8,128)}, f32[48,128]{1,0:T(8,128)}, u32[]{:S(2)}, u32[]{:S(2)}) collective-permute-start(f32[48,128]{1,0:T(8,128)} %add.144), channel_id=1, source_target_pairs={{0,8},{4,12},{8,0},{12,4},{16,24},{20,28},{24,16},{28,20},{1,9},{5... | collective-permute-start | bytes 73736 | tf_op jit(solution)/shard_map/cond/branch_8_fun/ppermute | solution.py:21
  82.6 15.6 %collective-permute-start.223 = (f32[488,128]{1,0:T(8,128)S(1)}, f32[488,128]{1,0:T(8,128)S(1)}, u32[]{:S(2)}, u32[]{:S(2)}) collective-permute-start(f32[488,128]{1,0:T(8,128)S(1)} %get-tuple-element.759.refs_0_), channel_id=1, source_target_pairs={{0,1},{1,0},{2,3},{3,2},{4,5},{5,4},{6,7},{7,6},{8,9},{9,8},{10,11... | collective-permute-start | bytes 749576 | tf_op jit(solution)/shard_map/ppermute | solution.py:21
  82.7 15.4 %collective-permute-start.224 = (f32[488,128]{1,0:T(8,128)}, f32[488,128]{1,0:T(8,128)S(1)}, u32[]{:S(2)}, u32[]{:S(2)}) collective-permute-start(f32[488,128]{1,0:T(8,128)} %get-tuple-element.760.refs_1_), channel_id=1, source_target_pairs={{0,1},{1,0},{2,3},{3,2},{4,5},{5,4},{6,7},{7,6},{8,9},{9,8},{10,11... | collective-permute-start | bytes 749576 | tf_op jit(solution)/shard_map/ppermute | solution.py:21
  83.1 17.0 %collective-permute-start.225 = (f32[488,128]{1,0:T(8,128)}, f32[488,128]{1,0:T(8,128)S(1)}, u32[]{:S(2)}, u32[]{:S(2)}) collective-permute-start(f32[488,128]{1,0:T(8,128)} %get-tuple-element.761.refs_1_), channel_id=1, source_target_pairs={{0,1},{1,0},{2,3},{3,2},{4,5},{5,4},{6,7},{7,6},{8,9},{9,8},{10,11... | collective-permute-start | bytes 749576 | tf_op jit(solution)/shard_map/ppermute | solution.py:21
  83.2 16.9 %collective-permute-start.226 = (f32[488,128]{1,0:T(8,128)}, f32[488,128]{1,0:T(8,128)S(1)}, u32[]{:S(2)}, u32[]{:S(2)}) collective-permute-start(f32[488,128]{1,0:T(8,128)} %get-tuple-element.762.refs_2_), channel_id=1, source_target_pairs={{0,1},{1,0},{2,3},{3,2},{4,5},{5,4},{6,7},{7,6},{8,9},{9,8},{10,11... | collective-permute-start | bytes 749576 | tf_op jit(solution)/shard_map/ppermute | solution.py:21
  87.8 10.3 %collective-permute-start.222 = (f32[48,128]{1,0:T(8,128)S(1)}, f32[48,128]{1,0:T(8,128)S(1)}, u32[]{:S(2)}, u32[]{:S(2)}) collective-permute-start(f32[48,128]{1,0:T(8,128)S(1)} %add.189), channel_id=1, source_target_pairs={{0,16},{4,20},{8,24},{12,28},{16,0},{20,4},{24,8},{28,12},{1,17},{... | collective-permute-start | bytes 73736 | tf_op jit(solution)/shard_map/ppermute | solution.py:21
  102.1 1.3 %collective-permute-start.227 = (f32[48,128]{1,0:T(8,128)S(1)}, f32[48,128]{1,0:T(8,128)S(1)}, u32[]{:S(2)}, u32[]{:S(2)}) collective-permute-start(f32[48,128]{1,0:T(8,128)S(1)} %add.190), channel_id=1, source_target_pairs={{0,1},{1,0},{2,3},{3,2},{4,5},{5,4},{6,7},{7,6},{8,9},{9,8},{10,11... | collective-permute-start | bytes 73736 | tf_op jit(solution)/shard_map/ppermute | solution.py:21
where the time goes:
time: 107 us; the launch traced here: 106 us
  starting transfers between devices  36.1 us (34%)
  waiting for transfers between devices  29.8 us (28%)
  Pallas kernels  29.5 us (28%)
  other arithmetic  4.82 us (5%)
  local copies, waits for them, and re-layouts  3.83 us (4%)
  between operations  2.09 us (2%)
    pallas_call x10, Pallas kernels, call(): pl.pallas_call(kernel, out_shape=out_shape, in_specs=in_specs or [VMEM] *...  29.5 us
    ppermute x17, starting transfers between devices, swap(): return lax.ppermute(x, axis, [(i, i ^ mask) for i in range(n)])  19.6 us
    ppermute x4, starting transfers between devices, shift(): return lax.ppermute(x, ('row', 'off'), route)  16.4 us
    ppermute x17, waiting for transfers between devices, swap(): return lax.ppermute(x, axis, [(i, i ^ mask) for i in range(n)])  15.2 us
    ppermute x4, waiting for transfers between devices, shift(): return lax.ppermute(x, ('row', 'off'), route)  14.6 us
  transfers between devices with their start and end apart: 21, of which 11 were waited for; matrix products, arithmetic and copies ran while one was open for 6% of the time, Pallas kernels for 14%

commit v1 on v0

--- a/solution.py
+++ b/solution.py
@@ -1,5 +1,4 @@
 import functools
-import itertools
 
 import jax
 import jax.numpy as jnp
@@ -21,14 +20,11 @@
     return lax.ppermute(x, axis, [(i, i ^ mask) for i in range(n)])
 
 
-def shift(x, distances):
-    rows, offs = lax.axis_size("row"), lax.axis_size("off")
-    if not any(distances):
+def shift(x, distance):
+    n = lax.axis_size("row")
+    if distance == 0:
         return x
-    route = [
-        (r * offs + o, (r + distances[o]) % rows * offs + o) for r in range(rows) for o in range(offs)
-    ]
-    return lax.ppermute(x, ("row", "off"), route)
+    return lax.ppermute(x, "row", [(i, (i + distance) % n) for i in range(n)])
 
 
 def after(x, *others):
@@ -111,6 +107,24 @@
         o_ref[pl.ds(8 * k, 8), :] = s
 
 
+def divide_kernel(t_ref, hi_ref, lo_ref):
+    t = t_ref[...]
+    hi = t.astype(BF16)
+    hi_ref[...] = hi
+    lo_ref[...] = (t - hi.astype(F32)).astype(BF16)
+
+
+def divide(tiles):
+    slots, width, _ = tiles.shape
+    step = max(s for s in (1, 2, 4, 8) if slots % s == 0)
+    spec = pl.BlockSpec((step, width, width), lambda i: (i, 0, 0))
+    shape = jax.ShapeDtypeStruct(tiles.shape, BF16)
+    return call(
+        divide_kernel, (shape, shape), (tiles,), [spec], 8,
+        flops=tiles.size * 4, grid=(slots // step,), out_specs=(spec, spec),
+    )
+
+
 def pick_kernel(vectors, slots, where_ref, at_ref, *refs):
     pieces, outs = refs[:-2], refs[-2:]
     for which, out in enumerate(outs):
@@ -125,14 +139,9 @@
             out[pl.ds(t * vectors, vectors), :] = value
 
 
-def split(x):
-    hi = x.astype(BF16)
-    return hi, (x - hi.astype(F32)).astype(BF16)
-
-
-def multiply_kernel(parts, step, transposed, x_refs, t_ref, o_ref):
+def multiply_kernel(parts, outs, step, transposed, x_refs, hi_ref, lo_ref, o_refs):
     base = pl.program_id(0) * step
-    width = o_ref.shape[-1]
+    width = hi_ref.shape[-1]
     vectors = sum(parts)
     dims = (((1,), (1 if transposed else 0,)), ((), ()))
 
@@ -145,31 +154,38 @@
         low = jnp.concatenate([lo, jnp.zeros_like(lo)], axis=1)
         return [top, low]
 
-    @pl.loop(0, step // 2)
+    def put(t, y):
+        first = 0
+        for ref, n in zip(o_refs, outs):
+            ref[pl.ds(t * n, n), :] = y[first : first + n]
+            first += n
+
+    @pl.loop(0, step // 2, unroll=2)
     def _(p):
         i = 2 * p
         x = jnp.concatenate(left(base + i) + left(base + i + 1), axis=0).astype(BF16)
         along, across = (1, 0) if transposed else (0, 1)
-        t = [jnp.concatenate(split(t_ref[i + k]), axis=along) for k in (0, 1)]
+        t = [jnp.concatenate([hi_ref[i + k], lo_ref[i + k]], axis=along) for k in (0, 1)]
         y = lax.dot_general(x, jnp.concatenate(t, axis=across), dims, preferred_element_type=F32)
-        o_ref[pl.ds((base + i) * vectors, vectors), :] = (y[0:8, :width] + y[8:16, :width])[:vectors]
-        o_ref[pl.ds((base + i + 1) * vectors, vectors), :] = (y[16:24, width:] + y[24:32, width:])[:vectors]
-
-
-def multiply(xs, tiles, ids, parts, transposed):
-    slots, width, _ = tiles.shape
+        put(base + i, y[0:8, :width] + y[8:16, :width])
+        put(base + i + 1, y[16:24, width:] + y[24:32, width:])
+
+
+def multiply(xs, high, low, ids, parts, outs, transposed):
+    slots, width, _ = high.shape
     step = max(s for s in (2, 4, 8, 16, 20) if slots % s == 0)
-    rows = sum(parts) * slots
     spec = pl.BlockSpec((step, width, width), lambda i: (i, 0, 0))
 
     def kernel(*refs):
-        x_refs, (t_ref, ids_ref, o_ref) = refs[: len(parts)], refs[len(parts) :]
-        multiply_kernel(parts, step, transposed, x_refs, t_ref, o_ref)
-        o_ref[pl.ds(rows, 8), :] = ids_ref[...]
+        x_refs, (hi_ref, lo_ref, ids_ref), o_refs = refs[: len(parts)], refs[len(parts) :][:3], refs[len(parts) + 3 :]
+        multiply_kernel(parts, outs, step, transposed, x_refs, hi_ref, lo_ref, o_refs)
+        for ref, n in zip(o_refs, outs):
+            ref[pl.ds(n * slots, 8), :] = ids_ref[...]
 
     return call(
-        kernel, jax.ShapeDtypeStruct((rows + 8, width), F32), (*xs, tiles, ids),
-        [VMEM] * len(parts) + [spec, VMEM], 12, flops=slots * 2 * 32 * 256 * 128, grid=(slots // step,), out_specs=VMEM,
+        kernel, tuple(jax.ShapeDtypeStruct((n * slots + 8, width), F32) for n in outs),
+        (*xs, high, low, ids), [VMEM] * len(parts) + [spec, spec, VMEM], 12,
+        flops=slots * 2 * 32 * 256 * 128, grid=(slots // step,),
     )
 
 
@@ -196,50 +212,44 @@
     o_ref[...] = jnp.broadcast_to(total, o_ref.shape)
 
 
-def add_kernel(vectors, slots, blocks, started, me_ref, *refs):
-    o_ref, hot_ref = refs[-2:]
-    lists = refs[:-2]
-    if started:
-        before, lists = lists[0], lists[1:]
+def add_kernel(shapes, slots, blocks, started, me_ref, *refs):
+    o_ref, refs = refs[-1], list(refs[:-1])
+    before = refs.pop(0) if started else None
+    lists = [[(refs.pop(0), n) for n in shape] for shape in shapes]
+    vectors = sum(shapes[0])
     width = o_ref.shape[-1]
     row = lax.broadcasted_iota(jnp.int32, (blocks, width), 0) + me_ref[0] * blocks
     row = row.astype(F32)
-    for k, ref in enumerate(lists):
-        ids = ref[vectors * slots : vectors * slots + 1, :]
-        hot_ref[:, k * width : (k + 1) * width] = jnp.where(ids == row, 1.0, 0.0).astype(BF16)
-    group = 2 if vectors % 2 == 0 else 1
-    pad = jnp.zeros((width - slots, group * width), F32)
-
-    @pl.loop(0, vectors // group)
-    def _(g):
-        sums = None
-        for k in range(0, len(lists), 2):
-            parts = []
-            for ref in lists[k : k + 2]:
-                y = [ref[pl.ds(g * group + v, slots, stride=vectors), :] for v in range(group)]
-                parts += [jnp.concatenate(y, axis=1), pad]
-            y = jnp.concatenate(parts, axis=0)
-            hi = y.astype(BF16)
-            lo = (y - hi.astype(F32)).astype(BF16)
-            hot = hot_ref[:, k * width : (k + 2) * width]
-            part = jnp.dot(hot, hi, preferred_element_type=F32) + jnp.dot(hot, lo, preferred_element_type=F32)
-            sums = part if sums is None else sums + part
-        for v in range(group):
-            at = pl.multiple_of((g * group + v) * blocks, 8)
-            s = sums[:, v * width : (v + 1) * width]
-            if started:
-                s = s + before[pl.ds(at, blocks), :]
-            o_ref[pl.ds(at, blocks), :] = s
-
-
-def add_lists(me, lists, vectors, slots, blocks, before=None):
-    width = lists[0].shape[-1]
-    operands = (me,) + (() if before is None else (before,)) + tuple(lists)
+    pad = jnp.zeros((width - slots, vectors * width), F32)
+    sums = None
+    for k in range(0, len(lists), 2):
+        hots, blocks_of = [], []
+        for parts in lists[k : k + 2]:
+            ref, n = parts[0]
+            ids = ref[n * slots : n * slots + 1, :]
+            hots.append(jnp.where(ids == row, 1.0, 0.0).astype(BF16))
+            blocks_of += [jnp.concatenate(load_each(parts, 0, slots), axis=1), pad]
+        hot = jnp.concatenate(hots, axis=1)
+        y = jnp.concatenate(blocks_of, axis=0)
+        hi = y.astype(BF16)
+        lo = (y - hi.astype(F32)).astype(BF16)
+        part = jnp.dot(hot, hi, preferred_element_type=F32) + jnp.dot(hot, lo, preferred_element_type=F32)
+        sums = part if sums is None else sums + part
+    for v in range(vectors):
+        s = sums[:, v * width : (v + 1) * width]
+        if started:
+            s = s + before[pl.ds(v * blocks, blocks), :]
+        o_ref[pl.ds(v * blocks, blocks), :] = s
+
+
+def add_lists(me, lists, slots, blocks, before=None):
+    width = lists[0][0].shape[-1]
+    shapes = [tuple(x.shape[0] // slots for x in parts) for parts in lists]
+    operands = (me,) + (() if before is None else (before,)) + tuple(x for parts in lists for x in parts)
     return call(
-        functools.partial(add_kernel, vectors, slots, blocks, before is not None),
-        jax.ShapeDtypeStruct((vectors * blocks, width), F32), operands,
-        [SMEM] + [VMEM] * (len(operands) - 1), 16,
-        scratch=(pltpu.VMEM((blocks, len(lists) * width), BF16),), flops=len(lists) * 2 * 256 * 256 * 768,
+        functools.partial(add_kernel, shapes, slots, blocks, before is not None),
+        jax.ShapeDtypeStruct((sum(shapes[0]) * blocks, width), F32), operands,
+        [SMEM] + [VMEM] * (len(operands) - 1), 16, flops=len(lists) * 2 * 256 * 256 * 768,
     )
 
 
@@ -350,24 +360,20 @@
 
     diagonal = diagonal.reshape(blocks, width)
 
-    arrangements = list(itertools.permutations(range(off_size))) if off_size <= 4 else []
-    listed = off_size == row_size // 2 and arrangements
-    if listed:
-        matches = jnp.all(jnp.array(arrangements, jnp.int32) == offset_map[None, :], axis=1)
-        which = jnp.argmax(matches).astype(jnp.int32)
+    offset = offset_map[me]
+    steps = row_size // 2
 
     def routed(function, *operands):
-        if listed:
-
-            def branch(distances):
-                return functools.partial(function, lambda x, sign: shift(x, [sign * d for d in distances]))
-
-            return lax.switch(which, [branch(a) for a in arrangements], *operands)
+        if steps <= 4:
+
+            def branch(s):
+                return functools.partial(function, lambda x, sign: shift(x, sign * s))
+
+            return lax.switch(offset, [branch(s) for s in range(steps)], *operands)
 
         def move(x, sign):
-            for b in range((row_size // 2).bit_length() - 1):
-                moved = shift(x, [sign << b] * off_size)
-                x = jnp.where(offset_map[me] >> b & 1 == 1, moved, x)
+            for b in range(steps.bit_length() - 1):
+                x = jnp.where(offset >> b & 1 == 1, shift(x, sign << b), x)
             return x
 
         return function(move, *operands)
@@ -387,42 +393,59 @@
             (where, at * n, *pieces), [SMEM, SMEM] + [VMEM] * off_size,
         )
 
-    inner = call(
-        functools.partial(inner_kernel, parts),
-        jax.ShapeDtypeStruct((16 * count, width), F32), (*packed, diagonal),
-    )
-    row0, col0 = pick(0, (where, at, inner))
-    arrived0 = routed(lambda move, x: move(x, -1), col0)
+    row0, col0 = pick(0, (where, at))
+
+    def first(move, col, packed, diagonal, tiles):
+        arrived = move(col, -1)
+        inner = call(
+            functools.partial(inner_kernel, parts),
+            jax.ShapeDtypeStruct((16 * count, width), F32), (*packed, diagonal),
+        )
+        high, low = divide(tiles)
+        return arrived, inner, high, low
+
+    arrived0, inner, high, low = routed(first, col0, packed, diagonal, tiles)
     row1, col1 = pick(1, (arrived0,))
 
-    def run(move, rows, arrived0, col1, inner, tiles, row_line, col_line):
+    def second(move, rows, arrived0, col1, high, low, row_line, col_line):
         arrived = [arrived0, move(col1, -1)]
-        mirrored = multiply(rows, tiles, col_line, parts, False)
+        mirrored, later = multiply(rows, high, low, col_line, parts, parts, False)
         returned = move(mirrored, 1)
-        direct = multiply(arrived, tiles, row_line, parts, True)
-        sums = call(
-            functools.partial(couple_kernel, parts, slots),
-            jax.ShapeDtypeStruct((-(-2 * count // 8) * 8, width), F32), (*rows, direct, inner),
-        )
-        stages = [sums]
-        for axis, bit in [("off", off_bits[0])] + [("row", b) for b in row_bits[:-1]]:
-            stages.append(sum_step(stages[-1], axis, bit))
-        direct_over = swap(after(direct, stages[0]), "off", off_bits[0])
-        returned_over = swap(after(returned, stages[1]), "off", off_bits[0])
-        return stages[-1], direct, direct_over, returned, returned_over
-
-    done = routed(run, [row0, row1], arrived0, col1, inner, tiles, row_line, col_line)
-    sums, direct, direct_over, returned, returned_over = done
+        (direct,) = multiply(arrived, high, low, row_line, parts, [vectors], True)
+        return direct, returned, later
+
+    rows = [row0, row1]
+    direct, returned, later = routed(second, rows, arrived0, col1, high, low, row_line, col_line)
+    sums = call(
+        functools.partial(couple_kernel, parts, slots),
+        jax.ShapeDtypeStruct((-(-2 * count // 8) * 8, width), F32), (*rows, direct, inner),
+    )
     top = off_bits[0]
+    partial_sums = sums
+    sums = sum_step(sums, "off", top)
+    direct_over = swap(after(direct, partial_sums), "off", top)
+    returned_over = swap(after(returned, partial_sums), "off", top)
+
+    def third(move, later, sums):
+        returned = move(later, 1)
+        for bit in row_bits[:-1]:
+            sums = sum_step(sums, "row", bit)
+        return returned, sums
+
+    later, sums = routed(third, later, sums)
+    later_over = swap(later, "off", top)
     sums = sum_step(sums, "row", row_bits[-1])
     direct = gather_off({0: direct, top: direct_over}, off_bits[1:])
     returned = gather_off({0: returned, top: returned_over}, off_bits[1:])
-    lists = [y for pair in zip(direct, returned) for y in pair]
-    image = add_lists(me[None], lists[:off_size], vectors, slots, blocks)
-    image = add_lists(me[None], lists[off_size:], vectors, slots, blocks, image)
+    later = gather_off({0: later, top: later_over}, off_bits[1:])
+    lists = []
+    for a, b, c in zip(direct, returned, later):
+        lists += [(a,), (b, c)]
+    image = add_lists(me[None], lists[:off_size], slots, blocks)
     sums = after(sums, image)
     for bit in off_bits[1:]:
         sums = sum_step(sums, "off", bit)
+    image = add_lists(me[None], lists[off_size:], slots, blocks, image)
     out = jax.ShapeDtypeStruct((vectors, shard), F32)
     return call(
         functools.partial(finish_kernel, parts, float(total)), (out, out),

time: 107 us -> 91.7 us (0.86)
  starting transfers between devices: 36.1 us -> 17.2 us
  Pallas kernels: 29.5 us -> 32.2 us
    ppermute x17 -> x20, starting transfers between devices: 19.6 us -> 9.52 us  [swap(): return lax.ppermute(x, axis, [(i, i ^ mask) for i in range(n)])]
    ppermute x4 -> x5, starting transfers between devices: 16.4 us -> 7.72 us  [shift(): return lax.ppermute(x, 'row', [(i, (i + distance) % n) for i in range(n)])]
    ppermute x17 -> x20, waiting for transfers between devices: 15.2 us -> 23.1 us  [swap(): return lax.ppermute(x, axis, [(i, i ^ mask) for i in range(n)])]
    ppermute x4 -> x5, waiting for transfers between devices: 14.6 us -> 7.63 us  [shift(): return lax.ppermute(x, 'row', [(i, (i + distance) % n) for i in range(n)])]
    pallas_call x10 -> x11, Pallas kernels: 29.5 us -> 32.2 us  [call(): pl.pallas_call(kernel, out_shape=out_shape, in_specs=in_specs or [VMEM] *...]
    dynamic_slice x0 -> x1, local copies, waits for them, and re-layouts: none -> 1.24 us  [body(): offset = offset_map[me]]
  transfers between devices with their start and end apart: 21 -> 25, of which waited for: 11 -> 10; matrix products, arithmetic and copies ran while one was open for 6% -> 7% of each run, Pallas kernels for 14% -> 24%
where the time goes in v1:
time: 91.7 us; the launch traced here: 91 us
  Pallas kernels  32.2 us (35%)
  waiting for transfers between devices  30.8 us (34%)
  starting transfers between devices  17.2 us (19%)
  local copies, waits for them, and re-layouts  4.62 us (5%)
  other arithmetic  3.96 us (4%)
  between operations  2.08 us (2%)
    pallas_call x11, Pallas kernels, call(): pl.pallas_call(kernel, out_shape=out_shape, in_specs=in_specs or [VMEM] *...  32.2 us
    ppermute x20, waiting for transfers between devices, swap(): return lax.ppermute(x, axis, [(i, i ^ mask) for i in range(n)])  23.1 us
    ppermute x20, starting transfers between devices, swap(): return lax.ppermute(x, axis, [(i, i ^ mask) for i in range(n)])  9.52 us
    ppermute x5, starting transfers between devices, shift(): return lax.ppermute(x, 'row', [(i, (i + distance) % n) for i in range(n)])  7.72 us
    ppermute x5, waiting for transfers between devices, shift(): return lax.ppermute(x, 'row', [(i, (i + distance) % n) for i in range(n)])  7.63 us
    unnamed x10, local copies, waits for them, and re-layouts  1.91 us
    convert_element_type x2, other arithmetic, padded(): ids.astype(F32)[None, :]  1.9 us
  transfers between devices with their start and end apart: 25, of which 10 were waited for; matrix products, arithmetic and copies ran while one was open for 7% of the time, Pallas kernels for 24%

profile of v1, /device:TPU:0, one launch (start us, length us, event | category | flops | bytes accessed | tf_op | source)
XLA Modules:
  0.0 91.0 jit_solution(12031076838183216399)
XLA Ops:
  0.6 1.2 %copy-done = f32[6,32768]{1,0:T(8,128)S(1)} copy-done((f32[6,32768]{1,0:T(8,128)S(1)}, f32[6,32768]{1,0:T(8,128)}, u32[]{:S(2)}) %copy-start) | copy-done | bytes 786456
  1.9 1.3 %shard_map.86 = (f32[768,128]{1,0:T(8,128)}, f32[768,128]{1,0:T(8,128)}) custom-call(f32[6,32768]{1,0:T(8,128)S(1)} %copy-done), custom_call_target="tpu_custom_call" | custom-call | bytes 786432 | tf_op jit(solution)/shard_map/pallas_call | solution.py:58
  3.2 3.0 %collective-permute-start.24 = (f32[768,128]{1,0:T(8,128)}, f32[768,128]{1,0:T(8,128)S(1)}, u32[]{:S(2)}, u32[]{:S(2)}) collective-permute-start(f32[768,128]{1,0:T(8,128)} %get-tuple-element.232.refs_0_), channel_id=1, source_target_pairs={{0,2},{1,3},{2,0},{3,1},{4,6},{5,7},{6,4},{7,5},{8,10},{9,11},{10,... | collective-permute-start | bytes 1179656 | tf_op jit(solution)/shard_map/ppermute | solution.py:20
  6.9 1.2 %fusion.2 = (f32[1,80]{1,0:T(1,128)}, s32[1,80]{1,0:T(1,128)S(1)}) fusion(s32[1,1,80]{2,1,0:T(1,128)} %param.26, s32[]{:T(128)} %bitcast.10), kind=kLoop, calls=%fused_computation.15 | loop fusion | flops 240 | bytes 964 | tf_op jit(solution)/shard_map/convert_element_type | solution.py:359
  8.8 1.2 %dynamic_slice.3 = s32[1]{0:T(128)} dynamic-slice(s32[4]{0:T(128)} %param.29, s32[]{:T(128)S(6)} %select_n.47), dynamic_slice_sizes={1} | dynamic-slice | bytes 12 | tf_op jit(solution)/shard_map/dynamic_slice | solution.py:363
  10.6 6.5 %conditional.4 = (f32[8,128]{1,0:T(8,128)}) conditional(s32[]{:T(128)} %bitcast, f32[8,128]{1,0:T(8,128)S(1)} %pad.9, f32[8,128]{1,0:T(8,128)S(1)} %pad.9, f32[8,128]{1,0:T(8,128)S(1)} %pad.9, f32[8,128]{1,0:T(8,128)S(1)} %pad.9), branch_computations={%region_0.1_spmd, %region_1.2_spmd, %region_2.3_spmd, %region_3.4_... | conditional | bytes 16432 | solution.py:372
  10.7 1.5 %collective-permute-start = (f32[8,128]{1,0:T(8,128)S(1)}, f32[8,128]{1,0:T(8,128)}, u32[]{:S(2)}, u32[]{:S(2)}) collective-permute-start(f32[8,128]{1,0:T(8,128)S(1)} %param.1), channel_id=1, source_target_pairs={{0,4},{4,8},{8,12},{12,16},{16,20},{20,24},{24,28},{28,0},{1,5},{5... | collective-permute-start | bytes 12296 | tf_op jit(solution)/shard_map/cond/branch_1_fun/ppermute | solution.py:27
  12.2 4.9 %collective-permute-done = f32[8,128]{1,0:T(8,128)} collective-permute-done((f32[8,128]{1,0:T(8,128)S(1)}, f32[8,128]{1,0:T(8,128)}, u32[]{:S(2)}, u32[]{:S(2)}) %collective-permute-start) | collective-permute-done | bytes 4128 | tf_op jit(solution)/shard_map/cond/branch_1_fun/ppermute | solution.py:27
  18.4 1.2 %collective-permute-done.25.refs_3_ = f32[768,128]{1,0:T(8,128)S(1)} collective-permute-done((f32[768,128]{1,0:T(8,128)S(1)}, f32[768,128]{1,0:T(8,128)S(1)}, u32[]{:S(2)}, u32[]{:S(2)}) %collective-permute-start.25) | collective-permute-done | bytes 393248 | tf_op jit(solution)/shard_map/ppermute | solution.py:20
  19.6 2.8 %shard_map.87 = (f32[240,128]{1,0:T(8,128)}, f32[240,128]{1,0:T(8,128)S(1)}) custom-call(s32[2,80]{1,0:T(2,128)S(1)} %get-tuple-element.257.where_ref, s32[2,80]{1,0:T(2,128)S(1)} %get-tuple-element.255.at_ref, f32[768,128]{1,0:T(8,128)} %get-tuple-element.232.refs_0_, f32[768,128]{1,0:T(8,128)S(1)} %collective-permute-done.23.refs_1_, ...), custom_call_target="tpu_custom_call" | custom-call | bytes 1574144 | tf_op jit(solution)/shard_map/pallas_call | solution.py:58
  22.4 11.8 %conditional.5 = (f32[240,128]{1,0:T(8,128)S(1)}, f32[336,128]{1,0:T(8,128)S(1)}, bf16[80,128,128]{2,1,0:T(8,128)(2,1)S(1)}, bf16[80,128,128]{2,1,0:T(8,128)(2,1)}) conditional(s32[]{:T(128)} %bitcast, (f32[768,128]{1,0:T(8,128)}, f32[768,128]{1,0:T(8,128)}, f32[256,128]{1,0:T(8,128)S(1)}, f32[80,128,128]{2,1,0:T(8,128)}, ...), branch_computations={%region_4.5_spmd, %region_5.6_spmd, %region_6.7_spmd, %region_7.8_... | conditional | flops 5242880 | bytes 6897736 | solution.py:372
  22.4 2.4 %collective-permute-start.3 = (f32[240,128]{1,0:T(8,128)S(1)}, f32[240,128]{1,0:T(8,128)S(1)}, u32[]{:S(2)}, u32[]{:S(2)}) collective-permute-start(f32[240,128]{1,0:T(8,128)S(1)} %get-tuple-element.140), channel_id=1, source_target_pairs={{0,28},{4,0},{8,4},{12,8},{16,12},{20,16},{24,20},{28,24},{1,29},{... | collective-permute-start | bytes 368648 | tf_op jit(solution)/shard_map/cond/branch_1_fun/ppermute | solution.py:27
  24.8 1.9 %branch_1_fun.4 = f32[336,128]{1,0:T(8,128)S(1)} custom-call(f32[768,128]{1,0:T(8,128)} %get-tuple-element.141.refs_0_, f32[768,128]{1,0:T(8,128)} %get-tuple-element.142.refs_1_, f32[256,128]{1,0:T(8,128)S(1)} %get-tuple-element.143.refs_2_), custom_call_target="tpu_custom_call" | custom-call | bytes 917504 | tf_op jit(solution)/shard_map/cond/branch_1_fun/pallas_call | solution.py:58
  26.7 7.5 %branch_1_fun.5 = (bf16[80,128,128]{2,1,0:T(8,128)(2,1)S(1)}, bf16[80,128,128]{2,1,0:T(8,128)(2,1)}) custom-call(f32[80,128,128]{2,1,0:T(8,128)} %get-tuple-element.144.t_ref), custom_call_target="tpu_custom_call" | custom-call | flops 5242880 | bytes 5242880 | tf_op jit(solution)/shard_map/cond/branch_1_fun/pallas_call | solution.py:58
  36.6 2.8 %shard_map.88 = (f32[240,128]{1,0:T(8,128)}, f32[240,128]{1,0:T(8,128)S(1)}) custom-call(s32[2,80]{1,0:T(2,128)S(1)} %get-tuple-element.257.where_ref, s32[2,80]{1,0:T(2,128)S(1)} %get-tuple-element.255.at_ref, f32[768,128]{1,0:T(8,128)} %get-tuple-element.235.refs_0_.refs_1_, f32[768,128]{1,0:T(8,128)S(1)} %collective-permute-done.26.refs_1_, ...), custom_call_target="tpu_custom_call" | custom-call | bytes 1574144 | tf_op jit(solution)/shard_map/pallas_call | solution.py:58
  39.4 13.4 %conditional.6 = (f32[488,128]{1,0:T(8,128)S(1)}, f32[248,128]{1,0:T(8,128)}, f32[248,128]{1,0:T(8,128)S(1)}) conditional(s32[]{:T(128)} %bitcast, (f32[240,128]{1,0:T(8,128)}, f32[240,128]{1,0:T(8,128)S(1)}, bf16[80,128,128]{2,1,0:T(8,128)(2,1)S(1)}, bf16[80,128,128]{2,1,0:T(8,128)(2,1)}, f32[8,128]{1,0:T(8,128)S(1)}, ...), branch_computations={%region_8.9_spmd, %region_9.10_spmd, %region_10.11_spmd, %region_1... | conditional | flops 335544320 | bytes 22962336 | solution.py:372
  40.3 4.8 %branch_1_fun.7 = (f32[248,128]{1,0:T(8,128)S(1)}, f32[248,128]{1,0:T(8,128)S(1)}) custom-call(f32[240,128]{1,0:T(8,128)} %get-tuple-element.176.refs_0_, f32[240,128]{1,0:T(8,128)} %get-tuple-element.177.refs_1_, bf16[80,128,128]{2,1,0:T(8,128)(2,1)S(1)} %get-tuple-element.173.refs_2_, bf16[80,128,128]{2,1,0:T(8,128)(2,1)} %get-tuple-element.174.refs_3_, ...), custom_call_target="tpu_custom_call" | custom-call | flops 167772160 | bytes 5492736 | tf_op jit(solution)/shard_map/cond/branch_1_fun/pallas_call | solution.py:58
  45.0 1.2 %collective-permute-start.7 = (f32[248,128]{1,0:T(8,128)S(1)}, f32[248,128]{1,0:T(8,128)}, u32[]{:S(2)}, u32[]{:S(2)}) collective-permute-start(f32[248,128]{1,0:T(8,128)S(1)} %get-tuple-element.179), channel_id=1, source_target_pairs={{0,4},{4,8},{8,12},{12,16},{16,20},{20,24},{24,28},{28,0},{1,5},{5... | collective-permute-start | bytes 380936 | tf_op jit(solution)/shard_map/cond/branch_1_fun/ppermute | solution.py:27
  46.3 3.9 %branch_1_fun.6 = f32[488,128]{1,0:T(8,128)S(1)} custom-call(f32[240,128]{1,0:T(8,128)S(1)} %copy-done.8, f32[240,128]{1,0:T(8,128)S(1)} %collective-permute-done.6.refs_1_, bf16[80,128,128]{2,1,0:T(8,128)(2,1)S(1)} %get-tuple-element.173.refs_2_, bf16[80,128,128]{2,1,0:T(8,128)(2,1)S(1)} %copy-done.2, f32[8,128]{1,0:T(8,128)S(1)} %get-tuple-element.175.refs_4_), custom_call_target="tpu_custom_call" | custom-call | flops 167772160 | bytes 5492736 | tf_op jit(solution)/shard_map/cond/branch_1_fun/pallas_call | solution.py:58
  50.1 2.7 %collective-permute-done.7 = f32[248,128]{1,0:T(8,128)} collective-permute-done((f32[248,128]{1,0:T(8,128)S(1)}, f32[248,128]{1,0:T(8,128)}, u32[]{:S(2)}, u32[]{:S(2)}) %collective-permute-start.7) | collective-permute-done | bytes 127008 | tf_op jit(solution)/shard_map/cond/branch_1_fun/ppermute | solution.py:27
  52.8 1.3 %shard_map.89 = f32[48,128]{1,0:T(8,128)S(1)} custom-call(f32[240,128]{1,0:T(8,128)} %get-tuple-element.234.refs_0_, f32[240,128]{1,0:T(8,128)} %get-tuple-element.239.refs_1_, f32[488,128]{1,0:T(8,128)S(1)} %get-tuple-element.251.refs_2_.refs_0_, f32[336,128]{1,0:T(8,128)S(1)} %copy-done.12), custom_call_target="tpu_custom_call" | custom-call | bytes 667648 | tf_op jit(solution)/shard_map/pallas_call | solution.py:58
  54.1 2.0 %collective-permute-start.36 = (f32[248,128]{1,0:T(8,128)}, f32[248,128]{1,0:T(8,128)S(1)}, u32[]{:S(2)}, u32[]{:S(2)}) collective-permute-start(f32[248,128]{1,0:T(8,128)} %get-tuple-element.252.refs_1_), channel_id=1, source_target_pairs={{0,2},{1,3},{2,0},{3,1},{4,6},{5,7},{6,4},{7,5},{8,10},{9,11},{10,... | collective-permute-start | bytes 380936 | tf_op jit(solution)/shard_map/ppermute | solution.py:20
  56.2 6.5 %collective-permute-done.29 = f32[48,128]{1,0:T(8,128)S(1)} collective-permute-done((f32[48,128]{1,0:T(8,128)S(1)}, f32[48,128]{1,0:T(8,128)S(1)}, u32[]{:S(2)}, u32[]{:S(2)}) %collective-permute-start.29) | collective-permute-done | bytes 24608 | tf_op jit(solution)/shard_map/ppermute | solution.py:20
  62.7 10.3 %conditional.7 = (f32[248,128]{1,0:T(8,128)S(1)}, f32[48,128]{1,0:T(8,128)}, f32[48,128]{1,0:T(8,128)S(1)}, f32[48,128]{1,0:T(8,128)}) conditional(s32[]{:T(128)} %bitcast, (f32[48,128]{1,0:T(8,128)S(1)}, f32[248,128]{1,0:T(8,128)S(1)}) %tuple.83, (f32[248,128]{1,0:T(8,128)S(1)}, f32[48,128]{1,0:T(8,128)S(1)}) %tuple.84, ...), branch_computations={%region_12.13_spmd, %region_13.14_spmd, %region_14.15_spmd, %regio... | conditional | flops 6144 | bytes 1081496 | solution.py:372
  62.7 1.7 %collective-permute-start.14 = (f32[248,128]{1,0:T(8,128)S(1)}, f32[248,128]{1,0:T(8,128)S(1)}, u32[]{:S(2)}, u32[]{:S(2)}) collective-permute-start(f32[248,128]{1,0:T(8,128)S(1)} %get-tuple-element.203), channel_id=1, source_target_pairs={{0,4},{4,8},{8,12},{12,16},{16,20},{20,24},{24,28},{28,0},{1,5},{5... | collective-permute-start | bytes 380936 | tf_op jit(solution)/shard_map/cond/branch_1_fun/ppermute | solution.py:27
  64.6 3.6 %collective-permute-done.15 = f32[48,128]{1,0:T(8,128)S(1)} collective-permute-done((f32[48,128]{1,0:T(8,128)S(1)}, f32[48,128]{1,0:T(8,128)S(1)}, u32[]{:S(2)}, u32[]{:S(2)}) %collective-permute-start.15) | collective-permute-done | bytes 24608 | tf_op jit(solution)/shard_map/cond/branch_1_fun/ppermute | solution.py:20
  68.8 1.2 %collective-permute-start.16 = (f32[48,128]{1,0:T(8,128)}, f32[48,128]{1,0:T(8,128)}, u32[]{:S(2)}, u32[]{:S(2)}) collective-permute-start(f32[48,128]{1,0:T(8,128)} %add.29), channel_id=1, source_target_pairs={{0,8},{4,12},{8,0},{12,4},{16,24},{20,28},{24,16},{28,20},{1,9},{5... | collective-permute-start | bytes 73736 | tf_op jit(solution)/shard_map/cond/branch_1_fun/ppermute | solution.py:20
  70.9 2.1 %collective-permute-done.16 = f32[48,128]{1,0:T(8,128)} collective-permute-done((f32[48,128]{1,0:T(8,128)}, f32[48,128]{1,0:T(8,128)}, u32[]{:S(2)}, u32[]{:S(2)}) %collective-permute-start.16) | collective-permute-done | bytes 24608 | tf_op jit(solution)/shard_map/cond/branch_1_fun/ppermute | solution.py:20
  74.8 3.6 %collective-permute-done.30 = f32[48,128]{1,0:T(8,128)S(1)} collective-permute-done((f32[48,128]{1,0:T(8,128)S(1)}, f32[48,128]{1,0:T(8,128)S(1)}, u32[]{:S(2)}, u32[]{:S(2)}) %collective-permute-start.30) | collective-permute-done | bytes 24608 | tf_op jit(solution)/shard_map/ppermute | solution.py:20
  79.2 4.2 %collective-permute-done.37.refs_3_ = f32[248,128]{1,0:T(8,128)S(1)} collective-permute-done((f32[248,128]{1,0:T(8,128)S(1)}, f32[248,128]{1,0:T(8,128)S(1)}, u32[]{:S(2)}, u32[]{:S(2)}) %collective-permute-start.37) | collective-permute-done | bytes 127008 | tf_op jit(solution)/shard_map/ppermute | solution.py:20
  83.4 1.5 %shard_map.90.refs_0_ = f32[1536,128]{1,0:T(8,128)S(1)} custom-call(s32[1]{0:T(128)} %bitcast.6.me_ref, f32[488,128]{1,0:T(8,128)S(1)} %get-tuple-element.251.refs_2_.refs_0_, f32[248,128]{1,0:T(8,128)} %get-tuple-element.252.refs_1_, f32[248,128]{1,0:T(8,128)S(1)} %get-tuple-element.249.refs_2_, f32[488,128]{1,0:T(8,128)S(1)} %collective-permute-done.31.refs_3_, ...), custom_call_target="tpu_custom_call" | custom-call | flops 402653184 | bytes 1007620 | tf_op jit(solution)/shard_map/pallas_call | solution.py:58
  86.9 4.0 %shard_map.92 = (f32[6,32768]{1,0:T(8,128)}, f32[6,32768]{1,0:T(8,128)}) custom-call(f32[48,128]{1,0:T(8,128)S(1)} %add.47.sums_ref, f32[768,128]{1,0:T(8,128)} %get-tuple-element.232.refs_0_, f32[768,128]{1,0:T(8,128)} %get-tuple-element.235.refs_0_.refs_1_, f32[256,128]{1,0:T(8,128)S(1)} %bitcast.20, f32[1536,128]{1,0:T(8,128)S(1)} %shard_map.91.refs_3_), custom_call_target="tpu_custom_call" | custom-call | bytes 1728512 | tf_op jit(solution)/shard_map/pallas_call | solution.py:58
  (62 shorter events, 11.5 us)
Async XLA Ops:
  0.6 1.2 %copy-start = (f32[6,32768]{1,0:T(8,128)S(1)}, f32[6,32768]{1,0:T(8,128)}, u32[]{:S(2)}) copy-start(f32[6,32768]{1,0:T(8,128)} %x_ref.1) | copy-start | bytes 2359300
  1.9 20.5 %copy-start.5 = (f32[32768]{0:T(1024)S(1)}, f32[32768]{0:T(1024)}, u32[]{:S(2)}) copy-start(f32[32768]{0:T(1024)} %param.24) | copy-start | bytes 393220
  3.2 14.6 %collective-permute-start.24 = (f32[768,128]{1,0:T(8,128)}, f32[768,128]{1,0:T(8,128)S(1)}, u32[]{:S(2)}, u32[]{:S(2)}) collective-permute-start(f32[768,128]{1,0:T(8,128)} %get-tuple-element.232.refs_0_), channel_id=1, source_target_pairs={{0,2},{1,3},{2,0},{3,1},{4,6},{5,7},{6,4},{7,5},{8,10},{9,11},{10,... | collective-permute-start | bytes 1179656 | tf_op jit(solution)/shard_map/ppermute | solution.py:20
  6.2 12.2 %collective-permute-start.23 = (f32[768,128]{1,0:T(8,128)}, f32[768,128]{1,0:T(8,128)S(1)}, u32[]{:S(2)}, u32[]{:S(2)}) collective-permute-start(f32[768,128]{1,0:T(8,128)} %get-tuple-element.232.refs_0_), channel_id=1, source_target_pairs={{0,1},{1,0},{2,3},{3,2},{4,5},{5,4},{6,7},{7,6},{8,9},{9,8},{10,11... | collective-permute-start | bytes 1179656 | tf_op jit(solution)/shard_map/ppermute | solution.py:20
  10.7 6.5 %collective-permute-start = (f32[8,128]{1,0:T(8,128)S(1)}, f32[8,128]{1,0:T(8,128)}, u32[]{:S(2)}, u32[]{:S(2)}) collective-permute-start(f32[8,128]{1,0:T(8,128)S(1)} %param.1), channel_id=1, source_target_pairs={{0,4},{4,8},{8,12},{12,16},{16,20},{20,24},{24,28},{28,0},{1,5},{5... | collective-permute-start | bytes 12296 | tf_op jit(solution)/shard_map/cond/branch_1_fun/ppermute | solution.py:27
  17.8 1.8 %collective-permute-start.25 = (f32[768,128]{1,0:T(8,128)S(1)}, f32[768,128]{1,0:T(8,128)S(1)}, u32[]{:S(2)}, u32[]{:S(2)}) collective-permute-start(f32[768,128]{1,0:T(8,128)S(1)} %collective-permute-done.24.refs_2_), channel_id=1, source_target_pairs={{0,1},{1,0},{2,3},{3,2},{4,5},{5,4},{6,7},{7,6},{8,9},{9,8},{10,11... | collective-permute-start | bytes 1179656 | tf_op jit(solution)/shard_map/ppermute | solution.py:20
  17.9 16.3 %collective-permute-start.27 = (f32[768,128]{1,0:T(8,128)}, f32[768,128]{1,0:T(8,128)S(1)}, u32[]{:S(2)}, u32[]{:S(2)}) collective-permute-start(f32[768,128]{1,0:T(8,128)} %get-tuple-element.235.refs_0_.refs_1_), channel_id=1, source_target_pairs={{0,2},{1,3},{2,0},{3,1},{4,6},{5,7},{6,4},{7,5},{8,10},{9,11},{10,... | collective-permute-start | bytes 1179656 | tf_op jit(solution)/shard_map/ppermute | solution.py:20
  18.0 17.6 %collective-permute-start.26 = (f32[768,128]{1,0:T(8,128)}, f32[768,128]{1,0:T(8,128)S(1)}, u32[]{:S(2)}, u32[]{:S(2)}) collective-permute-start(f32[768,128]{1,0:T(8,128)} %get-tuple-element.235.refs_0_.refs_1_), channel_id=1, source_target_pairs={{0,1},{1,0},{2,3},{3,2},{4,5},{5,4},{6,7},{7,6},{8,9},{9,8},{10,11... | collective-permute-start | bytes 1179656 | tf_op jit(solution)/shard_map/ppermute | solution.py:20
  22.4 11.7 %collective-permute-start.3 = (f32[240,128]{1,0:T(8,128)S(1)}, f32[240,128]{1,0:T(8,128)S(1)}, u32[]{:S(2)}, u32[]{:S(2)}) collective-permute-start(f32[240,128]{1,0:T(8,128)S(1)} %get-tuple-element.140), channel_id=1, source_target_pairs={{0,28},{4,0},{8,4},{12,8},{16,12},{20,16},{24,20},{28,24},{1,29},{... | collective-permute-start | bytes 368648 | tf_op jit(solution)/shard_map/cond/branch_1_fun/ppermute | solution.py:27
  34.2 0.6 copy-start.6
  34.2 0.7 copy-start.11
  34.9 1.7 %collective-permute-start.28 = (f32[768,128]{1,0:T(8,128)S(1)}, f32[768,128]{1,0:T(8,128)S(1)}, u32[]{:S(2)}, u32[]{:S(2)}) collective-permute-start(f32[768,128]{1,0:T(8,128)S(1)} %collective-permute-done.27.refs_2_), channel_id=1, source_target_pairs={{0,1},{1,0},{2,3},{3,2},{4,5},{5,4},{6,7},{7,6},{8,9},{9,8},{10,11... | collective-permute-start | bytes 1179656 | tf_op jit(solution)/shard_map/ppermute | solution.py:20
  39.4 13.4 %copy-start.12 = (f32[336,128]{1,0:T(8,128)S(1)}, f32[336,128]{1,0:T(8,128)}, u32[]{:S(2)}) copy-start(f32[336,128]{1,0:T(8,128)} %copy-done.11) | copy-start | bytes 516100
  39.4 6.9 %collective-permute-start.6 = (f32[240,128]{1,0:T(8,128)S(1)}, f32[240,128]{1,0:T(8,128)S(1)}, u32[]{:S(2)}, u32[]{:S(2)}) collective-permute-start(f32[240,128]{1,0:T(8,128)S(1)} %get-tuple-element.172), channel_id=1, source_target_pairs={{0,28},{4,0},{8,4},{12,8},{16,12},{20,16},{24,20},{28,24},{1,29},{... | collective-permute-start | bytes 368648 | tf_op jit(solution)/shard_map/cond/branch_1_fun/ppermute | solution.py:27
  40.3 6.0 %copy-start.2 = (bf16[80,128,128]{2,1,0:T(8,128)(2,1)S(1)}, bf16[80,128,128]{2,1,0:T(8,128)(2,1)}, u32[]{:S(2)}) copy-start(bf16[80,128,128]{2,1,0:T(8,128)(2,1)} %get-tuple-element.174.refs_3_) | copy-start | bytes 7864324 | tf_op jit(solution)/shard_map/cond
  40.3 6.0 %copy-start.8 = (f32[240,128]{1,0:T(8,128)S(1)}, f32[240,128]{1,0:T(8,128)}, u32[]{:S(2)}) copy-start(f32[240,128]{1,0:T(8,128)} %get-tuple-element.171.refs_0_) | copy-start | bytes 368644 | tf_op jit(solution)/shard_map/cond
  45.0 7.8 %collective-permute-start.7 = (f32[248,128]{1,0:T(8,128)S(1)}, f32[248,128]{1,0:T(8,128)}, u32[]{:S(2)}, u32[]{:S(2)}) collective-permute-start(f32[248,128]{1,0:T(8,128)S(1)} %get-tuple-element.179), channel_id=1, source_target_pairs={{0,4},{4,8},{8,12},{12,16},{16,20},{20,24},{24,28},{28,0},{1,5},{5... | collective-permute-start | bytes 380936 | tf_op jit(solution)/shard_map/cond/branch_1_fun/ppermute | solution.py:27
  54.1 24.5 %collective-permute-start.35 = (f32[488,128]{1,0:T(8,128)S(1)}, f32[488,128]{1,0:T(8,128)S(1)}, u32[]{:S(2)}, u32[]{:S(2)}) collective-permute-start(f32[488,128]{1,0:T(8,128)S(1)} %get-tuple-element.251.refs_2_.refs_0_), channel_id=1, source_target_pairs={{0,2},{1,3},{2,0},{3,1},{4,6},{5,7},{6,4},{7,5},{8,10},{9,11},{10,... | collective-permute-start | bytes 749576 | tf_op jit(solution)/shard_map/ppermute | solution.py:20
  54.1 24.5 %collective-permute-start.36 = (f32[248,128]{1,0:T(8,128)}, f32[248,128]{1,0:T(8,128)S(1)}, u32[]{:S(2)}, u32[]{:S(2)}) collective-permute-start(f32[248,128]{1,0:T(8,128)} %get-tuple-element.252.refs_1_), channel_id=1, source_target_pairs={{0,2},{1,3},{2,0},{3,1},{4,6},{5,7},{6,4},{7,5},{8,10},{9,11},{10,... | collective-permute-start | bytes 380936 | tf_op jit(solution)/shard_map/ppermute | solution.py:20
  56.1 27.3 %collective-permute-start.31 = (f32[488,128]{1,0:T(8,128)S(1)}, f32[488,128]{1,0:T(8,128)S(1)}, u32[]{:S(2)}, u32[]{:S(2)}) collective-permute-start(f32[488,128]{1,0:T(8,128)S(1)} %get-tuple-element.251.refs_2_.refs_0_), channel_id=1, source_target_pairs={{0,1},{1,0},{2,3},{3,2},{4,5},{5,4},{6,7},{7,6},{8,9},{9,8},{10,11... | collective-permute-start | bytes 749576 | tf_op jit(solution)/shard_map/ppermute | solution.py:20
  56.1 6.6 %collective-permute-start.29 = (f32[48,128]{1,0:T(8,128)S(1)}, f32[48,128]{1,0:T(8,128)S(1)}, u32[]{:S(2)}, u32[]{:S(2)}) collective-permute-start(f32[48,128]{1,0:T(8,128)S(1)} %shard_map.89), channel_id=1, source_target_pairs={{0,2},{1,3},{2,0},{3,1},{4,6},{5,7},{6,4},{7,5},{8,10},{9,11},{10,... | collective-permute-start | bytes 73736 | tf_op jit(solution)/shard_map/ppermute | solution.py:20
  62.7 8.2 %collective-permute-start.14 = (f32[248,128]{1,0:T(8,128)S(1)}, f32[248,128]{1,0:T(8,128)S(1)}, u32[]{:S(2)}, u32[]{:S(2)}) collective-permute-start(f32[248,128]{1,0:T(8,128)S(1)} %get-tuple-element.203), channel_id=1, source_target_pairs={{0,4},{4,8},{8,12},{12,16},{16,20},{20,24},{24,28},{28,0},{1,5},{5... | collective-permute-start | bytes 380936 | tf_op jit(solution)/shard_map/cond/branch_1_fun/ppermute | solution.py:27
  64.4 3.8 %collective-permute-start.15 = (f32[48,128]{1,0:T(8,128)S(1)}, f32[48,128]{1,0:T(8,128)S(1)}, u32[]{:S(2)}, u32[]{:S(2)}) collective-permute-start(f32[48,128]{1,0:T(8,128)S(1)} %get-tuple-element.204), channel_id=1, source_target_pairs={{0,4},{4,0},{8,12},{12,8},{16,20},{20,16},{24,28},{28,24},{1,5},{5... | collective-permute-start | bytes 73736 | tf_op jit(solution)/shard_map/cond/branch_1_fun/ppermute | solution.py:20
  68.8 4.1 %collective-permute-start.16 = (f32[48,128]{1,0:T(8,128)}, f32[48,128]{1,0:T(8,128)}, u32[]{:S(2)}, u32[]{:S(2)}) collective-permute-start(f32[48,128]{1,0:T(8,128)} %add.29), channel_id=1, source_target_pairs={{0,8},{4,12},{8,0},{12,4},{16,24},{20,28},{24,16},{28,20},{1,9},{5... | collective-permute-start | bytes 73736 | tf_op jit(solution)/shard_map/cond/branch_1_fun/ppermute | solution.py:20
  73.7 4.7 %collective-permute-start.30 = (f32[48,128]{1,0:T(8,128)S(1)}, f32[48,128]{1,0:T(8,128)S(1)}, u32[]{:S(2)}, u32[]{:S(2)}) collective-permute-start(f32[48,128]{1,0:T(8,128)S(1)} %add.45), channel_id=1, source_target_pairs={{0,16},{4,20},{8,24},{12,28},{16,0},{20,4},{24,8},{28,12},{1,17},{... | collective-permute-start | bytes 73736 | tf_op jit(solution)/shard_map/ppermute | solution.py:20
  74.8 4.3 %collective-permute-start.32 = (f32[248,128]{1,0:T(8,128)}, f32[248,128]{1,0:T(8,128)S(1)}, u32[]{:S(2)}, u32[]{:S(2)}) collective-permute-start(f32[248,128]{1,0:T(8,128)} %get-tuple-element.252.refs_1_), channel_id=1, source_target_pairs={{0,1},{1,0},{2,3},{3,2},{4,5},{5,4},{6,7},{7,6},{8,9},{9,8},{10,11... | collective-permute-start | bytes 380936 | tf_op jit(solution)/shard_map/ppermute | solution.py:20
  78.4 4.9 %collective-permute-start.37 = (f32[248,128]{1,0:T(8,128)S(1)}, f32[248,128]{1,0:T(8,128)S(1)}, u32[]{:S(2)}, u32[]{:S(2)}) collective-permute-start(f32[248,128]{1,0:T(8,128)S(1)} %get-tuple-element.249.refs_2_), channel_id=1, source_target_pairs={{0,2},{1,3},{2,0},{3,1},{4,6},{5,7},{6,4},{7,5},{8,10},{9,11},{10,... | collective-permute-start | bytes 380936 | tf_op jit(solution)/shard_map/ppermute | solution.py:20
  78.6 7.7 %collective-permute-start.38 = (f32[488,128]{1,0:T(8,128)S(1)}, f32[488,128]{1,0:T(8,128)S(1)}, u32[]{:S(2)}, u32[]{:S(2)}) collective-permute-start(f32[488,128]{1,0:T(8,128)S(1)} %collective-permute-done.35.refs_1_), channel_id=1, source_target_pairs={{0,1},{1,0},{2,3},{3,2},{4,5},{5,4},{6,7},{7,6},{8,9},{9,8},{10,11... | collective-permute-start | bytes 749576 | tf_op jit(solution)/shard_map/ppermute | solution.py:20
  78.6 4.8 %collective-permute-start.33 = (f32[248,128]{1,0:T(8,128)S(1)}, f32[248,128]{1,0:T(8,128)S(1)}, u32[]{:S(2)}, u32[]{:S(2)}) collective-permute-start(f32[248,128]{1,0:T(8,128)S(1)} %get-tuple-element.249.refs_2_), channel_id=1, source_target_pairs={{0,1},{1,0},{2,3},{3,2},{4,5},{5,4},{6,7},{7,6},{8,9},{9,8},{10,11... | collective-permute-start | bytes 380936 | tf_op jit(solution)/shard_map/ppermute | solution.py:20
  79.1 7.2 %collective-permute-start.39 = (f32[248,128]{1,0:T(8,128)S(1)}, f32[248,128]{1,0:T(8,128)S(1)}, u32[]{:S(2)}, u32[]{:S(2)}) collective-permute-start(f32[248,128]{1,0:T(8,128)S(1)} %collective-permute-done.36.refs_2_), channel_id=1, source_target_pairs={{0,1},{1,0},{2,3},{3,2},{4,5},{5,4},{6,7},{7,6},{8,9},{9,8},{10,11... | collective-permute-start | bytes 380936 | tf_op jit(solution)/shard_map/ppermute | solution.py:20
  83.4 2.9 %collective-permute-start.40 = (f32[248,128]{1,0:T(8,128)S(1)}, f32[248,128]{1,0:T(8,128)S(1)}, u32[]{:S(2)}, u32[]{:S(2)}) collective-permute-start(f32[248,128]{1,0:T(8,128)S(1)} %collective-permute-done.37.refs_3_), channel_id=1, source_target_pairs={{0,1},{1,0},{2,3},{3,2},{4,5},{5,4},{6,7},{7,6},{8,9},{9,8},{10,11... | collective-permute-start | bytes 380936 | tf_op jit(solution)/shard_map/ppermute | solution.py:20
  84.9 1.4 %collective-permute-start.34 = (f32[48,128]{1,0:T(8,128)S(1)}, f32[48,128]{1,0:T(8,128)S(1)}, u32[]{:S(2)}, u32[]{:S(2)}) collective-permute-start(f32[48,128]{1,0:T(8,128)S(1)} %add.46), channel_id=1, source_target_pairs={{0,1},{1,0},{2,3},{3,2},{4,5},{5,4},{6,7},{7,6},{8,9},{9,8},{10,11... | collective-permute-start | bytes 73736 | tf_op jit(solution)/shard_map/ppermute | solution.py:20

commit v2 on v1

--- a/solution.py
+++ b/solution.py
@@ -86,8 +86,13 @@
             first += n
 
 
-def inner_kernel(parts, *refs):
-    xs, (d_ref, o_ref) = list(zip(refs, parts)), refs[len(parts) :]
+def prepare_kernel(parts, slots, me_ref, count_ref, map_ref, rows_ref, cols_ref, *refs):
+    xs, (d_ref, ids_ref, offset_ref, o_ref) = list(zip(refs, parts)), refs[len(parts) :]
+    offset_ref[0] = map_ref[me_ref[0]]
+    live = lax.broadcasted_iota(jnp.int32, (1, slots), 1) < count_ref[0, 0]
+    ids_ref[...] = jnp.full(ids_ref.shape, -1, jnp.int32)
+    ids_ref[0:1, :slots] = jnp.where(live, rows_ref[...], -1)
+    ids_ref[1:2, :slots] = jnp.where(live, cols_ref[...], -1)
     vectors = sum(parts)
     blocks, width = d_ref.shape
     both = pairs(vectors)
@@ -125,14 +130,17 @@
     )
 
 
-def pick_kernel(vectors, slots, where_ref, at_ref, *refs):
+def pick_kernel(vectors, slots, blocks, me_ref, own_ref, other_ref, *refs):
     pieces, outs = refs[:-2], refs[-2:]
-    for which, out in enumerate(outs):
+    me = me_ref[0]
+    for ids_ref, line, out in ((own_ref, 0, outs[0]), (other_ref, 1, outs[1])):
 
         @pl.loop(0, slots, unroll=4)
         def _(t):
-            m = where_ref[which, t]
-            at = at_ref[which, t]
+            b = ids_ref[line, t]
+            place = jnp.maximum(b, 0)
+            m = jnp.where(b < 0, -1, (place // blocks) ^ me)
+            at = (place % blocks) * vectors
             value = jnp.zeros((vectors, out.shape[-1]), F32)
             for k, piece in enumerate(pieces):
                 value = jnp.where(m == k, piece[pl.ds(at, vectors), :], value)
@@ -171,7 +179,7 @@
         put(base + i + 1, y[16:24, width:] + y[24:32, width:])
 
 
-def multiply(xs, high, low, ids, parts, outs, transposed):
+def multiply(xs, high, low, ids, line, parts, outs, transposed):
     slots, width, _ = high.shape
     step = max(s for s in (2, 4, 8, 16, 20) if slots % s == 0)
     spec = pl.BlockSpec((step, width, width), lambda i: (i, 0, 0))
@@ -180,7 +188,7 @@
         x_refs, (hi_ref, lo_ref, ids_ref), o_refs = refs[: len(parts)], refs[len(parts) :][:3], refs[len(parts) + 3 :]
         multiply_kernel(parts, outs, step, transposed, x_refs, hi_ref, lo_ref, o_refs)
         for ref, n in zip(o_refs, outs):
-            ref[pl.ds(n * slots, 8), :] = ids_ref[...]
+            ref[pl.ds(n * slots, 8), :] = jnp.broadcast_to(ids_ref[line : line + 1, :], (8, width)).astype(F32)
 
     return call(
         kernel, tuple(jax.ShapeDtypeStruct((n * slots + 8, width), F32) for n in outs),
@@ -335,7 +343,6 @@
 
 def body(start_block, diagonal, tile_values, tile_rows, tile_cols, tile_counts, offset_map):
     tiles = tile_values[0, 0]
-    live_count = tile_counts[0, 0]
     row_size = lax.axis_size("row")
     off_size = lax.axis_size("off")
     me = lax.axis_index("off").astype(jnp.int32)
@@ -351,16 +358,18 @@
         functools.partial(pack_kernel, parts, blocks),
         tuple(jax.ShapeDtypeStruct((n * blocks, width), F32) for n in parts), (start_block,),
     )
-    live = jnp.arange(slots, dtype=jnp.int32) < live_count
-    row_ids = jnp.where(live, tile_rows[0, 0], -1)
-    col_ids = jnp.where(live, tile_cols[0, 0], -1)
-
-    def padded(ids):
-        return jnp.pad(ids.astype(F32)[None, :], ((0, 7), (0, width - slots)), constant_values=-1)
-
     diagonal = diagonal.reshape(blocks, width)
-
-    offset = offset_map[me]
+    ids, offset, inner = call(
+        functools.partial(prepare_kernel, parts, slots),
+        (
+            jax.ShapeDtypeStruct((8, width), jnp.int32),
+            jax.ShapeDtypeStruct((1,), jnp.int32),
+            jax.ShapeDtypeStruct((16 * count, width), F32),
+        ),
+        (me[None], tile_counts, offset_map, tile_rows[0], tile_cols[0], *packed, diagonal),
+        [SMEM] * 3 + [VMEM] * (3 + len(parts)), out_specs=(VMEM, SMEM, VMEM),
+    )
+    offset = offset[0]
     steps = row_size // 2
 
     def routed(function, *operands):
@@ -378,44 +387,31 @@
 
         return function(move, *operands)
 
-    row_line, col_line = padded(row_ids), padded(col_ids)
-    group_line = routed(lambda move, x: move(x, 1), col_line)
-    both = jnp.stack([row_ids, group_line[0, :slots].astype(jnp.int32)])
-    where = jnp.where(both < 0, -1, (both // blocks) ^ me)
-    at = jnp.where(both < 0, 0, both % blocks)
+    group_ids = routed(lambda move, x: move(x, 1), ids)
+    high, low = divide(tiles)
 
     def pick(k, hold):
         n = parts[k]
         pieces = gather_off({0: packed[k]}, off_bits, hold)
         picked = jax.ShapeDtypeStruct((n * slots, width), F32)
         return call(
-            functools.partial(pick_kernel, n, slots), (picked, picked),
-            (where, at * n, *pieces), [SMEM, SMEM] + [VMEM] * off_size,
+            functools.partial(pick_kernel, n, slots, blocks), (picked, picked),
+            (me[None], ids, group_ids, *pieces), [SMEM] * 3 + [VMEM] * off_size,
         )
 
-    row0, col0 = pick(0, (where, at))
-
-    def first(move, col, packed, diagonal, tiles):
-        arrived = move(col, -1)
-        inner = call(
-            functools.partial(inner_kernel, parts),
-            jax.ShapeDtypeStruct((16 * count, width), F32), (*packed, diagonal),
-        )
-        high, low = divide(tiles)
-        return arrived, inner, high, low
-
-    arrived0, inner, high, low = routed(first, col0, packed, diagonal, tiles)
+    row0, col0 = pick(0, (group_ids, high, low))
+    arrived0 = routed(lambda move, x: move(x, -1), col0)
     row1, col1 = pick(1, (arrived0,))
 
-    def second(move, rows, arrived0, col1, high, low, row_line, col_line):
+    def second(move, rows, arrived0, col1, high, low, ids):
         arrived = [arrived0, move(col1, -1)]
-        mirrored, later = multiply(rows, high, low, col_line, parts, parts, False)
+        mirrored, later = multiply(rows, high, low, ids, 1, parts, parts, False)
         returned = move(mirrored, 1)
-        (direct,) = multiply(arrived, high, low, row_line, parts, [vectors], True)
+        (direct,) = multiply(arrived, high, low, ids, 0, parts, [vectors], True)
         return direct, returned, later
 
     rows = [row0, row1]
-    direct, returned, later = routed(second, rows, arrived0, col1, high, low, row_line, col_line)
+    direct, returned, later = routed(second, rows, arrived0, col1, high, low, ids)
     sums = call(
         functools.partial(couple_kernel, parts, slots),
         jax.ShapeDtypeStruct((-(-2 * count // 8) * 8, width), F32), (*rows, direct, inner),
@@ -437,7 +433,7 @@
     sums = sum_step(sums, "row", row_bits[-1])
     direct = gather_off({0: direct, top: direct_over}, off_bits[1:])
     returned = gather_off({0: returned, top: returned_over}, off_bits[1:])
-    later = gather_off({0: later, top: later_over}, off_bits[1:])
+    later = gather_off({0: later, top: later_over}, off_bits[1:], (sums,))
     lists = []
     for a, b, c in zip(direct, returned, later):
         lists += [(a,), (b, c)]

time: 91.7 us -> 89.1 us (0.972)
  Pallas kernels: 32.2 us -> 26 us
  waiting for transfers between devices: 30.8 us -> 36 us
  local copies, waits for them, and re-layouts: 4.62 us -> 7.37 us
  other arithmetic: 3.96 us -> 1.37 us
  starting transfers between devices: 17.2 us -> 15.7 us
    pallas_call x11, Pallas kernels: 32.2 us -> 26 us  [call(): pl.pallas_call(kernel, out_shape=out_shape, in_specs=in_specs or [VMEM] *...]
    ppermute x5, waiting for transfers between devices: 7.63 us -> 13.4 us  [shift(): return lax.ppermute(x, 'row', [(i, (i + distance) % n) for i in range(n)])]
    unnamed x10 -> x14, local copies, waits for them, and re-layouts: 1.91 us -> 6.57 us
    convert_element_type x3 -> x0, other arithmetic: 2.58 us -> none  [the longest x2 1.9 us: padded(): ids.astype(F32)[None, :]]
    ppermute x20, starting transfers between devices: 9.52 us -> 8.14 us  [swap(): return lax.ppermute(x, axis, [(i, i ^ mask) for i in range(n)])]
    dynamic_slice x1 -> x0, local copies, waits for them, and re-layouts: 1.24 us -> none  [body(): offset = offset_map[me]]
  transfers between devices with their start and end apart: 25 -> 25, of which waited for: 10 -> 15; matrix products, arithmetic and copies ran while one was open for 7% -> 2% of each run, Pallas kernels for 24% -> 22%
where the time goes in v2:
time: 89.1 us; the launch traced here: 88.6 us
  waiting for transfers between devices  36 us (40%)
  Pallas kernels  26 us (29%)
  starting transfers between devices  15.7 us (18%)
  local copies, waits for them, and re-layouts  7.37 us (8%)
  between operations  2.06 us (2%)
  other arithmetic  1.37 us (2%)
    pallas_call x11, Pallas kernels, call(): pl.pallas_call(kernel, out_shape=out_shape, in_specs=in_specs or [VMEM] *...  26 us
    ppermute x20, waiting for transfers between devices, swap(): return lax.ppermute(x, axis, [(i, i ^ mask) for i in range(n)])  22.6 us
    ppermute x5, waiting for transfers between devices, shift(): return lax.ppermute(x, 'row', [(i, (i + distance) % n) for i in range(n)])  13.4 us
    ppermute x20, starting transfers between devices, swap(): return lax.ppermute(x, axis, [(i, i ^ mask) for i in range(n)])  8.14 us
    ppermute x5, starting transfers between devices, shift(): return lax.ppermute(x, 'row', [(i, (i + distance) % n) for i in range(n)])  7.56 us
    unnamed x14, local copies, waits for them, and re-layouts  6.57 us
  transfers between devices with their start and end apart: 25, of which 15 were waited for; matrix products, arithmetic and copies ran while one was open for 2% of the time, Pallas kernels for 22%

profile of v2, /device:TPU:0, one launch (start us, length us, event | category | flops | bytes accessed | tf_op | source)
XLA Modules:
  0.0 88.6 jit_solution(902572903650846437)
XLA Ops:
  0.6 1.2 %copy-done.1 = f32[6,32768]{1,0:T(8,128)S(1)} copy-done((f32[6,32768]{1,0:T(8,128)S(1)}, f32[6,32768]{1,0:T(8,128)}, u32[]{:S(2)}) %copy-start.1) | copy-done | bytes 786456
  2.3 3.1 %collective-permute-start.24 = (f32[768,128]{1,0:T(8,128)S(1)}, f32[768,128]{1,0:T(8,128)S(1)}, u32[]{:S(2)}, u32[]{:S(2)}) collective-permute-start(f32[768,128]{1,0:T(8,128)S(1)} %get-tuple-element.163.refs_0_), channel_id=1, source_target_pairs={{0,2},{1,3},{2,0},{3,1},{4,6},{5,7},{6,4},{7,5},{8,10},{9,11},{10,... | collective-permute-start | bytes 1179656 | tf_op jit(solution)/shard_map/ppermute | solution.py:20
  8.9 1.8 %shard_map.87 = (s32[8,128]{1,0:T(8,128)S(1)}, s32[1]{0:T(128)}, f32[336,128]{1,0:T(8,128)S(1)}) custom-call(s32[1]{0:T(128)} %bitcast.me_ref, s32[1,1]{1,0:T(1,128)S(6)} %copy.49.count_ref, s32[4]{0:T(128)S(1)} %copy-done.4, s32[1,80]{1,0:T(1,128)S(1)} %bitcast.9, s32[1,80]{1,0:T(1,128)S(1)} %bitcast.10, f32[768,128]{1,0:T(8,128)S(1)} %get-tuple-element.163.refs_0_, ...), custom_call_target="tpu_custom_call" | custom-call | bytes 918168 | tf_op jit(solution)/shard_map/pallas_call | solution.py:58
  11.4 6.5 %conditional.4 = (s32[8,128]{1,0:T(8,128)}) conditional(s32[]{:T(128)} %bitcast.4, s32[8,128]{1,0:T(8,128)S(1)} %get-tuple-element.166.own_ref, s32[8,128]{1,0:T(8,128)S(1)} %get-tuple-element.166.own_ref, s32[8,128]{1,0:T(8,128)S(1)} %get-tuple-element.166.own_ref, s32[8,128]{1,0:T(8,128)S(1)} %get-tuple-element.166.own_ref), branch_computations={%region_0.0_spmd, %region_1.0_spmd, %region_2.0_spmd, %region_3.0_... | conditional | bytes 16432 | solution.py:381
  11.4 1.5 %collective-permute-start = (s32[8,128]{1,0:T(8,128)S(1)}, s32[8,128]{1,0:T(8,128)}, u32[]{:S(2)}, u32[]{:S(2)}) collective-permute-start(s32[8,128]{1,0:T(8,128)S(1)} %param.1), channel_id=1, source_target_pairs={{0,4},{4,8},{8,12},{12,16},{16,20},{20,24},{24,28},{28,0},{1,5},{5... | collective-permute-start | bytes 12296 | tf_op jit(solution)/shard_map/cond/branch_1_fun/ppermute | solution.py:27
  12.9 4.9 %collective-permute-done = s32[8,128]{1,0:T(8,128)} collective-permute-done((s32[8,128]{1,0:T(8,128)S(1)}, s32[8,128]{1,0:T(8,128)}, u32[]{:S(2)}, u32[]{:S(2)}) %collective-permute-start) | collective-permute-done | bytes 4128 | tf_op jit(solution)/shard_map/cond/branch_1_fun/ppermute | solution.py:27
  17.9 2.5 %copy-done = f32[1,1,80,128,128]{4,3,2,1,0:T(8,128)S(1)} copy-done((f32[1,1,80,128,128]{4,3,2,1,0:T(8,128)S(1)}, f32[1,1,80,128,128]{4,3,2,1,0:T(8,128)}, u32[]{:S(2)}) %copy-start) | copy-done | bytes 5242904
  20.3 4.4 %shard_map.88 = (bf16[80,128,128]{2,1,0:T(8,128)(2,1)}, bf16[80,128,128]{2,1,0:T(8,128)(2,1)}) custom-call(f32[80,128,128]{2,1,0:T(8,128)S(1)} %bitcast.6), custom_call_target="tpu_custom_call" | custom-call | flops 5242880 | bytes 5242880 | tf_op jit(solution)/shard_map/pallas_call | solution.py:58
  25.3 1.2 %collective-permute-done.25.refs_3_ = f32[768,128]{1,0:T(8,128)S(1)} collective-permute-done((f32[768,128]{1,0:T(8,128)S(1)}, f32[768,128]{1,0:T(8,128)S(1)}, u32[]{:S(2)}, u32[]{:S(2)}) %collective-permute-start.25) | collective-permute-done | bytes 393248 | tf_op jit(solution)/shard_map/ppermute | solution.py:20
  26.5 2.5 %shard_map.89 = (f32[240,128]{1,0:T(8,128)S(1)}, f32[240,128]{1,0:T(8,128)S(1)}) custom-call(s32[1]{0:T(128)} %bitcast.me_ref, s32[8,128]{1,0:T(8,128)S(1)} %get-tuple-element.166.own_ref, s32[8,128]{1,0:T(8,128)} %get-tuple-element.230.other_ref, f32[768,128]{1,0:T(8,128)S(1)} %get-tuple-element.163.refs_0_, ...), custom_call_target="tpu_custom_call" | custom-call | bytes 1581060 | tf_op jit(solution)/shard_map/pallas_call | solution.py:58
  29.0 5.0 %conditional.5 = (f32[240,128]{1,0:T(8,128)S(1)}) conditional(s32[]{:T(128)} %bitcast.4, f32[240,128]{1,0:T(8,128)S(1)} %get-tuple-element.171, f32[240,128]{1,0:T(8,128)S(1)} %get-tuple-element.171, f32[240,128]{1,0:T(8,128)S(1)} %get-tuple-element.171, f32[240,128]{1,0:T(8,128)S(1)} %get-tuple-element.171), branch_computations={%region_4.0_spmd, %region_5.0_spmd, %region_6.0_spmd, %region_7.0_... | conditional | bytes 737328 | solution.py:381
  29.0 1.9 %collective-permute-start.3 = (f32[240,128]{1,0:T(8,128)S(1)}, f32[240,128]{1,0:T(8,128)S(1)}, u32[]{:S(2)}, u32[]{:S(2)}) collective-permute-start(f32[240,128]{1,0:T(8,128)S(1)} %param.5), channel_id=1, source_target_pairs={{0,28},{4,0},{8,4},{12,8},{16,12},{20,16},{24,20},{28,24},{1,29},{... | collective-permute-start | bytes 368648 | tf_op jit(solution)/shard_map/cond/branch_1_fun/ppermute | solution.py:27
  30.9 3.0 %collective-permute-done.3 = f32[240,128]{1,0:T(8,128)S(1)} collective-permute-done((f32[240,128]{1,0:T(8,128)S(1)}, f32[240,128]{1,0:T(8,128)S(1)}, u32[]{:S(2)}, u32[]{:S(2)}) %collective-permute-start.3) | collective-permute-done | bytes 122912 | tf_op jit(solution)/shard_map/cond/branch_1_fun/ppermute | solution.py:27
  34.0 2.3 %collective-permute-done.27.refs_2_ = f32[768,128]{1,0:T(8,128)S(1)} collective-permute-done((f32[768,128]{1,0:T(8,128)S(1)}, f32[768,128]{1,0:T(8,128)S(1)}, u32[]{:S(2)}, u32[]{:S(2)}) %collective-permute-start.27) | collective-permute-done | bytes 393248 | tf_op jit(solution)/shard_map/ppermute | solution.py:20
  36.3 1.7 %collective-permute-done.28.refs_3_ = f32[768,128]{1,0:T(8,128)S(1)} collective-permute-done((f32[768,128]{1,0:T(8,128)S(1)}, f32[768,128]{1,0:T(8,128)S(1)}, u32[]{:S(2)}, u32[]{:S(2)}) %collective-permute-start.28) | collective-permute-done | bytes 393248 | tf_op jit(solution)/shard_map/ppermute | solution.py:20
  38.0 2.5 %shard_map.90 = (f32[240,128]{1,0:T(8,128)S(1)}, f32[240,128]{1,0:T(8,128)S(1)}) custom-call(s32[1]{0:T(128)} %bitcast.me_ref, s32[8,128]{1,0:T(8,128)S(1)} %get-tuple-element.166.own_ref, s32[8,128]{1,0:T(8,128)} %get-tuple-element.230.other_ref, f32[768,128]{1,0:T(8,128)S(1)} %get-tuple-element.164.refs_1_.refs_0_, ...), custom_call_target="tpu_custom_call" | custom-call | bytes 1581060 | tf_op jit(solution)/shard_map/pallas_call | solution.py:58
  40.5 15.8 %conditional.6 = (f32[488,128]{1,0:T(8,128)S(1)}, f32[248,128]{1,0:T(8,128)}, f32[248,128]{1,0:T(8,128)S(1)}) conditional(s32[]{:T(128)} %bitcast.4, (f32[240,128]{1,0:T(8,128)S(1)}, f32[240,128]{1,0:T(8,128)S(1)}, bf16[80,128,128]{2,1,0:T(8,128)(2,1)}, bf16[80,128,128]{2,1,0:T(8,128)(2,1)}, s32[8,128]{1,0:T(8,128)S(1)}, ...), branch_computations={%region_8.0_spmd, %region_9.0_spmd, %region_10.0_spmd, %region_11.... | conditional | flops 335544320 | bytes 32956576 | solution.py:381
  40.6 2.8 %collective-permute-start.6 = (f32[240,128]{1,0:T(8,128)S(1)}, f32[240,128]{1,0:T(8,128)S(1)}, u32[]{:S(2)}, u32[]{:S(2)}) collective-permute-start(f32[240,128]{1,0:T(8,128)S(1)} %get-tuple-element.104), channel_id=1, source_target_pairs={{0,28},{4,0},{8,4},{12,8},{16,12},{20,16},{24,20},{28,24},{1,29},{... | collective-permute-start | bytes 368648 | tf_op jit(solution)/shard_map/cond/branch_1_fun/ppermute | solution.py:27
  43.3 5.2 %branch_1_fun.3 = (f32[248,128]{1,0:T(8,128)S(1)}, f32[248,128]{1,0:T(8,128)S(1)}) custom-call(f32[240,128]{1,0:T(8,128)S(1)} %get-tuple-element.108.refs_0_, f32[240,128]{1,0:T(8,128)S(1)} %get-tuple-element.109.refs_1_, bf16[80,128,128]{2,1,0:T(8,128)(2,1)} %get-tuple-element.105.refs_2_, bf16[80,128,128]{2,1,0:T(8,128)(2,1)} %get-tuple-element.106.refs_3_, ...), custom_call_target="tpu_custom_call" | custom-call | flops 167772160 | bytes 5492736 | tf_op jit(solution)/shard_map/cond/branch_1_fun/pallas_call | solution.py:58
  48.6 3.8 %branch_1_fun.2 = f32[488,128]{1,0:T(8,128)S(1)} custom-call(f32[240,128]{1,0:T(8,128)S(1)} %get-tuple-element.103.refs_0_, f32[240,128]{1,0:T(8,128)S(1)} %collective-permute-done.6.refs_1_, bf16[80,128,128]{2,1,0:T(8,128)(2,1)S(1)} %copy-done.8, bf16[80,128,128]{2,1,0:T(8,128)(2,1)S(1)} %copy-done.12, s32[8,128]{1,0:T(8,128)S(1)} %get-tuple-element.107.refs_4_), custom_call_target="tpu_custom_call" | custom-call | flops 167772160 | bytes 5492736 | tf_op jit(solution)/shard_map/cond/branch_1_fun/pallas_call | solution.py:58
  52.5 3.9 %collective-permute-done.7 = f32[248,128]{1,0:T(8,128)} collective-permute-done((f32[248,128]{1,0:T(8,128)S(1)}, f32[248,128]{1,0:T(8,128)}, u32[]{:S(2)}, u32[]{:S(2)}) %collective-permute-start.7) | collective-permute-done | bytes 127008 | tf_op jit(solution)/shard_map/cond/branch_1_fun/ppermute | solution.py:27
  56.6 2.0 %collective-permute-start.36 = (f32[248,128]{1,0:T(8,128)}, f32[248,128]{1,0:T(8,128)S(1)}, u32[]{:S(2)}, u32[]{:S(2)}) collective-permute-start(f32[248,128]{1,0:T(8,128)} %get-tuple-element.184.refs_1_), channel_id=1, source_target_pairs={{0,2},{1,3},{2,0},{3,1},{4,6},{5,7},{6,4},{7,5},{8,10},{9,11},{10,... | collective-permute-start | bytes 380936 | tf_op jit(solution)/shard_map/ppermute | solution.py:20
  58.7 6.0 %collective-permute-done.29 = f32[48,128]{1,0:T(8,128)S(1)} collective-permute-done((f32[48,128]{1,0:T(8,128)S(1)}, f32[48,128]{1,0:T(8,128)S(1)}, u32[]{:S(2)}, u32[]{:S(2)}) %collective-permute-start.29) | collective-permute-done | bytes 24608 | tf_op jit(solution)/shard_map/ppermute | solution.py:20
  64.8 9.9 %conditional.7 = (f32[248,128]{1,0:T(8,128)S(1)}, f32[48,128]{1,0:T(8,128)}, f32[48,128]{1,0:T(8,128)S(1)}, f32[48,128]{1,0:T(8,128)}) conditional(s32[]{:T(128)} %bitcast.4, (f32[48,128]{1,0:T(8,128)S(1)}, f32[248,128]{1,0:T(8,128)S(1)}) %tuple.78, (f32[248,128]{1,0:T(8,128)S(1)}, ...), branch_computations={%region_12.0_spmd, %region_13.0_spmd, %region_14.0_spmd, %region_1... | conditional | flops 6144 | bytes 1081496 | solution.py:381
  64.8 1.3 %collective-permute-start.14 = (f32[248,128]{1,0:T(8,128)S(1)}, f32[248,128]{1,0:T(8,128)S(1)}, u32[]{:S(2)}, u32[]{:S(2)}) collective-permute-start(f32[248,128]{1,0:T(8,128)S(1)} %get-tuple-element.132), channel_id=1, source_target_pairs={{0,4},{4,8},{8,12},{12,16},{16,20},{20,24},{24,28},{28,0},{1,5},{5... | collective-permute-start | bytes 380936 | tf_op jit(solution)/shard_map/cond/branch_1_fun/ppermute | solution.py:27
  66.2 3.7 %collective-permute-done.15 = f32[48,128]{1,0:T(8,128)S(1)} collective-permute-done((f32[48,128]{1,0:T(8,128)S(1)}, f32[48,128]{1,0:T(8,128)S(1)}, u32[]{:S(2)}, u32[]{:S(2)}) %collective-permute-start.15) | collective-permute-done | bytes 24608 | tf_op jit(solution)/shard_map/cond/branch_1_fun/ppermute | solution.py:20
  71.3 1.5 %collective-permute-done.14 = f32[248,128]{1,0:T(8,128)S(1)} collective-permute-done((f32[248,128]{1,0:T(8,128)S(1)}, f32[248,128]{1,0:T(8,128)S(1)}, u32[]{:S(2)}, u32[]{:S(2)}) %collective-permute-start.14) | collective-permute-done | bytes 127008 | tf_op jit(solution)/shard_map/cond/branch_1_fun/ppermute | solution.py:27
  72.9 1.8 %collective-permute-done.16 = f32[48,128]{1,0:T(8,128)} collective-permute-done((f32[48,128]{1,0:T(8,128)}, f32[48,128]{1,0:T(8,128)}, u32[]{:S(2)}, u32[]{:S(2)}) %collective-permute-start.16) | collective-permute-done | bytes 24608 | tf_op jit(solution)/shard_map/cond/branch_1_fun/ppermute | solution.py:20
  75.4 1.2 %collective-permute-start.30 = (f32[48,128]{1,0:T(8,128)S(1)}, f32[48,128]{1,0:T(8,128)S(1)}, u32[]{:S(2)}, u32[]{:S(2)}) collective-permute-start(f32[48,128]{1,0:T(8,128)S(1)} %add.29), channel_id=1, source_target_pairs={{0,16},{4,20},{8,24},{12,28},{16,0},{20,4},{24,8},{28,12},{1,17},{... | collective-permute-start | bytes 73736 | tf_op jit(solution)/shard_map/ppermute | solution.py:20
  76.7 3.5 %collective-permute-done.30 = f32[48,128]{1,0:T(8,128)S(1)} collective-permute-done((f32[48,128]{1,0:T(8,128)S(1)}, f32[48,128]{1,0:T(8,128)S(1)}, u32[]{:S(2)}, u32[]{:S(2)}) %collective-permute-start.30) | collective-permute-done | bytes 24608 | tf_op jit(solution)/shard_map/ppermute | solution.py:20
  82.3 1.5 %shard_map.92.refs_0_ = f32[1536,128]{1,0:T(8,128)S(1)} custom-call(s32[1]{0:T(128)} %bitcast.me_ref, f32[488,128]{1,0:T(8,128)S(1)} %get-tuple-element.183.refs_2_.refs_0_, f32[248,128]{1,0:T(8,128)} %get-tuple-element.184.refs_1_, f32[248,128]{1,0:T(8,128)S(1)} %get-tuple-element.181.refs_2_, f32[488,128]{1,0:T(8,128)S(1)} %collective-permute-done.31.refs_3_, ...), custom_call_target="tpu_custom_call" | custom-call | flops 402653184 | bytes 1007620 | tf_op jit(solution)/shard_map/pallas_call | solution.py:58
  85.7 2.9 %shard_map.94 = (f32[6,32768]{1,0:T(8,128)}, f32[6,32768]{1,0:T(8,128)}) custom-call(f32[48,128]{1,0:T(8,128)S(1)} %add.31.sums_ref, f32[768,128]{1,0:T(8,128)S(1)} %get-tuple-element.163.refs_0_, f32[768,128]{1,0:T(8,128)S(1)} %get-tuple-element.164.refs_1_.refs_0_, f32[256,128]{1,0:T(8,128)S(1)} %bitcast.8, f32[1536,128]{1,0:T(8,128)S(1)} %shard_map.93.refs_3_), custom_call_target="tpu_custom_call" | custom-call | bytes 1728512 | tf_op jit(solution)/shard_map/pallas_call | solution.py:58
  (59 shorter events, 10.5 us)
Async XLA Ops:
  0.6 1.2 %copy-start.1 = (f32[6,32768]{1,0:T(8,128)S(1)}, f32[6,32768]{1,0:T(8,128)}, u32[]{:S(2)}) copy-start(f32[6,32768]{1,0:T(8,128)} %x_ref.1) | copy-start | bytes 2359300
  2.3 22.5 %collective-permute-start.24 = (f32[768,128]{1,0:T(8,128)S(1)}, f32[768,128]{1,0:T(8,128)S(1)}, u32[]{:S(2)}, u32[]{:S(2)}) collective-permute-start(f32[768,128]{1,0:T(8,128)S(1)} %get-tuple-element.163.refs_0_), channel_id=1, source_target_pairs={{0,2},{1,3},{2,0},{3,1},{4,6},{5,7},{6,4},{7,5},{8,10},{9,11},{10,... | collective-permute-start | bytes 1179656 | tf_op jit(solution)/shard_map/ppermute | solution.py:20
  5.4 19.9 %collective-permute-start.23 = (f32[768,128]{1,0:T(8,128)S(1)}, f32[768,128]{1,0:T(8,128)S(1)}, u32[]{:S(2)}, u32[]{:S(2)}) collective-permute-start(f32[768,128]{1,0:T(8,128)S(1)} %get-tuple-element.163.refs_0_), channel_id=1, source_target_pairs={{0,1},{1,0},{2,3},{3,2},{4,5},{5,4},{6,7},{7,6},{8,9},{9,8},{10,11... | collective-permute-start | bytes 1179656 | tf_op jit(solution)/shard_map/ppermute | solution.py:20
  6.0 0.9 %copy-start.2 = (f32[32768]{0:T(1024)S(1)}, f32[32768]{0:T(1024)}, u32[]{:S(2)}) copy-start(f32[32768]{0:T(1024)} %param.24) | copy-start | bytes 393220
  6.9 0.7 copy-start.4
  11.4 6.5 %collective-permute-start = (s32[8,128]{1,0:T(8,128)S(1)}, s32[8,128]{1,0:T(8,128)}, u32[]{:S(2)}, u32[]{:S(2)}) collective-permute-start(s32[8,128]{1,0:T(8,128)S(1)} %param.1), channel_id=1, source_target_pairs={{0,4},{4,8},{8,12},{12,16},{16,20},{20,24},{24,28},{28,0},{1,5},{5... | collective-permute-start | bytes 12296 | tf_op jit(solution)/shard_map/cond/branch_1_fun/ppermute | solution.py:27
  17.8 2.5 %copy-start = (f32[1,1,80,128,128]{4,3,2,1,0:T(8,128)S(1)}, f32[1,1,80,128,128]{4,3,2,1,0:T(8,128)}, u32[]{:S(2)}) copy-start(f32[1,1,80,128,128]{4,3,2,1,0:T(8,128)} %param.25) | copy-start | bytes 15728644
  24.8 1.7 %collective-permute-start.25 = (f32[768,128]{1,0:T(8,128)S(1)}, f32[768,128]{1,0:T(8,128)S(1)}, u32[]{:S(2)}, u32[]{:S(2)}) collective-permute-start(f32[768,128]{1,0:T(8,128)S(1)} %collective-permute-done.24.refs_2_), channel_id=1, source_target_pairs={{0,1},{1,0},{2,3},{3,2},{4,5},{5,4},{6,7},{7,6},{8,9},{9,8},{10,11... | collective-permute-start | bytes 1179656 | tf_op jit(solution)/shard_map/ppermute | solution.py:20
  24.8 11.5 %collective-permute-start.27 = (f32[768,128]{1,0:T(8,128)S(1)}, f32[768,128]{1,0:T(8,128)S(1)}, u32[]{:S(2)}, u32[]{:S(2)}) collective-permute-start(f32[768,128]{1,0:T(8,128)S(1)} %get-tuple-element.164.refs_1_.refs_0_), channel_id=1, source_target_pairs={{0,2},{1,3},{2,0},{3,1},{4,6},{5,7},{6,4},{7,5},{8,10},{9,11},{10,... | collective-permute-start | bytes 1179656 | tf_op jit(solution)/shard_map/ppermute | solution.py:20
  24.9 11.5 %collective-permute-start.26 = (f32[768,128]{1,0:T(8,128)S(1)}, f32[768,128]{1,0:T(8,128)S(1)}, u32[]{:S(2)}, u32[]{:S(2)}) collective-permute-start(f32[768,128]{1,0:T(8,128)S(1)} %get-tuple-element.164.refs_1_.refs_0_), channel_id=1, source_target_pairs={{0,1},{1,0},{2,3},{3,2},{4,5},{5,4},{6,7},{7,6},{8,9},{9,8},{10,11... | collective-permute-start | bytes 1179656 | tf_op jit(solution)/shard_map/ppermute | solution.py:20
  29.0 4.9 %collective-permute-start.3 = (f32[240,128]{1,0:T(8,128)S(1)}, f32[240,128]{1,0:T(8,128)S(1)}, u32[]{:S(2)}, u32[]{:S(2)}) collective-permute-start(f32[240,128]{1,0:T(8,128)S(1)} %param.5), channel_id=1, source_target_pairs={{0,28},{4,0},{8,4},{12,8},{16,12},{20,16},{24,20},{28,24},{1,29},{... | collective-permute-start | bytes 368648 | tf_op jit(solution)/shard_map/cond/branch_1_fun/ppermute | solution.py:27
  36.3 1.7 %collective-permute-start.28 = (f32[768,128]{1,0:T(8,128)S(1)}, f32[768,128]{1,0:T(8,128)S(1)}, u32[]{:S(2)}, u32[]{:S(2)}) collective-permute-start(f32[768,128]{1,0:T(8,128)S(1)} %collective-permute-done.27.refs_2_), channel_id=1, source_target_pairs={{0,1},{1,0},{2,3},{3,2},{4,5},{5,4},{6,7},{7,6},{8,9},{9,8},{10,11... | collective-permute-start | bytes 1179656 | tf_op jit(solution)/shard_map/ppermute | solution.py:20
  40.6 8.1 %collective-permute-start.6 = (f32[240,128]{1,0:T(8,128)S(1)}, f32[240,128]{1,0:T(8,128)S(1)}, u32[]{:S(2)}, u32[]{:S(2)}) collective-permute-start(f32[240,128]{1,0:T(8,128)S(1)} %get-tuple-element.104), channel_id=1, source_target_pairs={{0,28},{4,0},{8,4},{12,8},{16,12},{20,16},{24,20},{28,24},{1,29},{... | collective-permute-start | bytes 368648 | tf_op jit(solution)/shard_map/cond/branch_1_fun/ppermute | solution.py:27
  43.3 5.3 %copy-start.8 = (bf16[80,128,128]{2,1,0:T(8,128)(2,1)S(1)}, bf16[80,128,128]{2,1,0:T(8,128)(2,1)}, u32[]{:S(2)}) copy-start(bf16[80,128,128]{2,1,0:T(8,128)(2,1)} %get-tuple-element.105.refs_2_) | copy-start | bytes 7864324 | tf_op jit(solution)/shard_map/cond
  43.3 5.3 %copy-start.12 = (bf16[80,128,128]{2,1,0:T(8,128)(2,1)S(1)}, bf16[80,128,128]{2,1,0:T(8,128)(2,1)}, u32[]{:S(2)}) copy-start(bf16[80,128,128]{2,1,0:T(8,128)(2,1)} %get-tuple-element.106.refs_3_) | copy-start | bytes 7864324 | tf_op jit(solution)/shard_map/cond
  48.5 7.8 %collective-permute-start.7 = (f32[248,128]{1,0:T(8,128)S(1)}, f32[248,128]{1,0:T(8,128)}, u32[]{:S(2)}, u32[]{:S(2)}) collective-permute-start(f32[248,128]{1,0:T(8,128)S(1)} %get-tuple-element.110), channel_id=1, source_target_pairs={{0,4},{4,8},{8,12},{12,16},{16,20},{20,24},{24,28},{28,0},{1,5},{5... | collective-permute-start | bytes 380936 | tf_op jit(solution)/shard_map/cond/branch_1_fun/ppermute | solution.py:27
  56.6 23.6 %collective-permute-start.35 = (f32[488,128]{1,0:T(8,128)S(1)}, f32[488,128]{1,0:T(8,128)S(1)}, u32[]{:S(2)}, u32[]{:S(2)}) collective-permute-start(f32[488,128]{1,0:T(8,128)S(1)} %get-tuple-element.183.refs_2_.refs_0_), channel_id=1, source_target_pairs={{0,2},{1,3},{2,0},{3,1},{4,6},{5,7},{6,4},{7,5},{8,10},{9,11},{10,... | collective-permute-start | bytes 749576 | tf_op jit(solution)/shard_map/ppermute | solution.py:20
  56.6 24.1 %collective-permute-start.36 = (f32[248,128]{1,0:T(8,128)}, f32[248,128]{1,0:T(8,128)S(1)}, u32[]{:S(2)}, u32[]{:S(2)}) collective-permute-start(f32[248,128]{1,0:T(8,128)} %get-tuple-element.184.refs_1_), channel_id=1, source_target_pairs={{0,2},{1,3},{2,0},{3,1},{4,6},{5,7},{6,4},{7,5},{8,10},{9,11},{10,... | collective-permute-start | bytes 380936 | tf_op jit(solution)/shard_map/ppermute | solution.py:20
  58.7 23.6 %collective-permute-start.31 = (f32[488,128]{1,0:T(8,128)S(1)}, f32[488,128]{1,0:T(8,128)S(1)}, u32[]{:S(2)}, u32[]{:S(2)}) collective-permute-start(f32[488,128]{1,0:T(8,128)S(1)} %get-tuple-element.183.refs_2_.refs_0_), channel_id=1, source_target_pairs={{0,1},{1,0},{2,3},{3,2},{4,5},{5,4},{6,7},{7,6},{8,9},{9,8},{10,11... | collective-permute-start | bytes 749576 | tf_op jit(solution)/shard_map/ppermute | solution.py:20
  58.7 6.1 %collective-permute-start.29 = (f32[48,128]{1,0:T(8,128)S(1)}, f32[48,128]{1,0:T(8,128)S(1)}, u32[]{:S(2)}, u32[]{:S(2)}) collective-permute-start(f32[48,128]{1,0:T(8,128)S(1)} %shard_map.91), channel_id=1, source_target_pairs={{0,2},{1,3},{2,0},{3,1},{4,6},{5,7},{6,4},{7,5},{8,10},{9,11},{10,... | collective-permute-start | bytes 73736 | tf_op jit(solution)/shard_map/ppermute | solution.py:20
  64.8 20.9 %copy-start.3 = (f32[32768]{0:T(1024)S(1)}, f32[32768]{0:T(1024)}, u32[]{:S(2)}) copy-start(f32[32768]{0:T(1024)} %param.24) | copy-start | bytes 393220
  64.8 8.1 %collective-permute-start.14 = (f32[248,128]{1,0:T(8,128)S(1)}, f32[248,128]{1,0:T(8,128)S(1)}, u32[]{:S(2)}, u32[]{:S(2)}) collective-permute-start(f32[248,128]{1,0:T(8,128)S(1)} %get-tuple-element.132), channel_id=1, source_target_pairs={{0,4},{4,8},{8,12},{12,16},{16,20},{20,24},{24,28},{28,0},{1,5},{5... | collective-permute-start | bytes 380936 | tf_op jit(solution)/shard_map/cond/branch_1_fun/ppermute | solution.py:27
  66.1 3.8 %collective-permute-start.15 = (f32[48,128]{1,0:T(8,128)S(1)}, f32[48,128]{1,0:T(8,128)S(1)}, u32[]{:S(2)}, u32[]{:S(2)}) collective-permute-start(f32[48,128]{1,0:T(8,128)S(1)} %get-tuple-element.133), channel_id=1, source_target_pairs={{0,4},{4,0},{8,12},{12,8},{16,20},{20,16},{24,28},{28,24},{1,5},{5... | collective-permute-start | bytes 73736 | tf_op jit(solution)/shard_map/cond/branch_1_fun/ppermute | solution.py:20
  70.5 4.1 %collective-permute-start.16 = (f32[48,128]{1,0:T(8,128)}, f32[48,128]{1,0:T(8,128)}, u32[]{:S(2)}, u32[]{:S(2)}) collective-permute-start(f32[48,128]{1,0:T(8,128)} %add.18), channel_id=1, source_target_pairs={{0,8},{4,12},{8,0},{12,4},{16,24},{20,28},{24,16},{28,20},{1,9},{5... | collective-permute-start | bytes 73736 | tf_op jit(solution)/shard_map/cond/branch_1_fun/ppermute | solution.py:20
  75.4 4.8 %collective-permute-start.30 = (f32[48,128]{1,0:T(8,128)S(1)}, f32[48,128]{1,0:T(8,128)S(1)}, u32[]{:S(2)}, u32[]{:S(2)}) collective-permute-start(f32[48,128]{1,0:T(8,128)S(1)} %add.29), channel_id=1, source_target_pairs={{0,16},{4,20},{8,24},{12,28},{16,0},{20,4},{24,8},{28,12},{1,17},{... | collective-permute-start | bytes 73736 | tf_op jit(solution)/shard_map/ppermute | solution.py:20
  76.7 4.9 %collective-permute-start.37 = (f32[248,128]{1,0:T(8,128)S(1)}, f32[248,128]{1,0:T(8,128)S(1)}, u32[]{:S(2)}, u32[]{:S(2)}) collective-permute-start(f32[248,128]{1,0:T(8,128)S(1)} %get-tuple-element.181.refs_2_), channel_id=1, source_target_pairs={{0,2},{1,3},{2,0},{3,1},{4,6},{5,7},{6,4},{7,5},{8,10},{9,11},{10,... | collective-permute-start | bytes 380936 | tf_op jit(solution)/shard_map/ppermute | solution.py:20
  80.2 1.6 %collective-permute-start.32 = (f32[248,128]{1,0:T(8,128)}, f32[248,128]{1,0:T(8,128)S(1)}, u32[]{:S(2)}, u32[]{:S(2)}) collective-permute-start(f32[248,128]{1,0:T(8,128)} %get-tuple-element.184.refs_1_), channel_id=1, source_target_pairs={{0,1},{1,0},{2,3},{3,2},{4,5},{5,4},{6,7},{7,6},{8,9},{9,8},{10,11... | collective-permute-start | bytes 380936 | tf_op jit(solution)/shard_map/ppermute | solution.py:20
  80.2 4.9 %collective-permute-start.38 = (f32[488,128]{1,0:T(8,128)S(1)}, f32[488,128]{1,0:T(8,128)S(1)}, u32[]{:S(2)}, u32[]{:S(2)}) collective-permute-start(f32[488,128]{1,0:T(8,128)S(1)} %collective-permute-done.35.refs_1_), channel_id=1, source_target_pairs={{0,1},{1,0},{2,3},{3,2},{4,5},{5,4},{6,7},{7,6},{8,9},{9,8},{10,11... | collective-permute-start | bytes 749576 | tf_op jit(solution)/shard_map/ppermute | solution.py:20
  80.7 1.6 %collective-permute-start.33 = (f32[248,128]{1,0:T(8,128)S(1)}, f32[248,128]{1,0:T(8,128)S(1)}, u32[]{:S(2)}, u32[]{:S(2)}) collective-permute-start(f32[248,128]{1,0:T(8,128)S(1)} %get-tuple-element.181.refs_2_), channel_id=1, source_target_pairs={{0,1},{1,0},{2,3},{3,2},{4,5},{5,4},{6,7},{7,6},{8,9},{9,8},{10,11... | collective-permute-start | bytes 380936 | tf_op jit(solution)/shard_map/ppermute | solution.py:20
  81.6 3.5 %collective-permute-start.39 = (f32[248,128]{1,0:T(8,128)S(1)}, f32[248,128]{1,0:T(8,128)S(1)}, u32[]{:S(2)}, u32[]{:S(2)}) collective-permute-start(f32[248,128]{1,0:T(8,128)S(1)} %collective-permute-done.36.refs_2_), channel_id=1, source_target_pairs={{0,1},{1,0},{2,3},{3,2},{4,5},{5,4},{6,7},{7,6},{8,9},{9,8},{10,11... | collective-permute-start | bytes 380936 | tf_op jit(solution)/shard_map/ppermute | solution.py:20
  81.8 3.3 %collective-permute-start.40 = (f32[248,128]{1,0:T(8,128)S(1)}, f32[248,128]{1,0:T(8,128)S(1)}, u32[]{:S(2)}, u32[]{:S(2)}) collective-permute-start(f32[248,128]{1,0:T(8,128)S(1)} %collective-permute-done.37.refs_3_), channel_id=1, source_target_pairs={{0,1},{1,0},{2,3},{3,2},{4,5},{5,4},{6,7},{7,6},{8,9},{9,8},{10,11... | collective-permute-start | bytes 380936 | tf_op jit(solution)/shard_map/ppermute | solution.py:20
  83.8 1.3 %collective-permute-start.34 = (f32[48,128]{1,0:T(8,128)S(1)}, f32[48,128]{1,0:T(8,128)S(1)}, u32[]{:S(2)}, u32[]{:S(2)}) collective-permute-start(f32[48,128]{1,0:T(8,128)S(1)} %add.30), channel_id=1, source_target_pairs={{0,1},{1,0},{2,3},{3,2},{4,5},{5,4},{6,7},{7,6},{8,9},{9,8},{10,11... | collective-permute-start | bytes 73736 | tf_op jit(solution)/shard_map/ppermute | solution.py:20
  (2 other events, 1.3 us)
